TPU v7x, 32 devices: a whole 2x2x4 slice. The times are simulated.
32 devices in a mesh: seq: 2 (over x), fsdp: 16 (over z, y, core).
Axes of the slice: x: 2, y: 2, z: 4, core: 2. Of those that a mesh axis runs over, the one named last changes fastest.
Arguments:
- tokens_in: bfloat16 [32, 2048, 768], P('fsdp', 'seq')
- segment_ids: int32 [32, 2048], P('fsdp'), may hold values from 0 to 15, never falling along the last dimension, each value on 1 to 1024 neighbouring positions
- random_blocks: int32 [32, 32, 3], P('fsdp'), may hold values from 0 to 31
- global_blocks: int32 [32, 2], P('fsdp'), may hold values from 0 to 31
- w_query: bfloat16 [768, 768], P('fsdp'), may hold values from -0.15625 to 0.15625
- b_query: bfloat16 [768], P('fsdp'), may hold values from -1.5 to 1.5
- w_key: bfloat16 [768, 768], P('fsdp'), may hold values from -0.15625 to 0.15625
- w_value: bfloat16 [768, 768], P('fsdp'), may hold values from -0.21875 to 0.21875
- b_value: bfloat16 [768], P('fsdp'), may hold values from -1.5 to 1.5
- w_attn_out: bfloat16 [768, 768], P('fsdp'), may hold values from -0.875 to 0.875
- b_attn_out: bfloat16 [768], P('fsdp'), may hold values from -1.5 to 1.5
- ln1_gain: bfloat16 [768], P('fsdp'), may hold values from 0.5 to 1.5
- ln1_bias: bfloat16 [768], P('fsdp'), may hold values from -1.5 to 1.5
- w_inner: bfloat16 [768, 3072], P('fsdp')
- b_inner: bfloat16 [3072], P('fsdp'), may hold values from -1.5 to 1.5
- w_outer: bfloat16 [3072, 768], P('fsdp'), may hold values from -0.109375 to 0.109375
- b_outer: bfloat16 [768], P('fsdp'), may hold values from -1.5 to 1.5
- ln2_gain: bfloat16 [768], P('fsdp'), may hold values from 0.5 to 1.5
- ln2_bias: bfloat16 [768], P('fsdp'), may hold values from -1.5 to 1.5
- out_grad: bfloat16 [32, 2048, 768], P('fsdp', 'seq'), may hold values from -6 to 6
Outputs:
- out_tokens: bfloat16 [32, 2048, 768], P('fsdp', 'seq')
- d_tokens_in: bfloat16 [32, 2048, 768], P('fsdp', 'seq')
- d_w_query: float32 [768, 768], P('fsdp')
- d_b_query: float32 [768], P('fsdp')
- d_w_key: float32 [768, 768], P('fsdp')
- d_w_value: float32 [768, 768], P('fsdp')
- d_b_value: float32 [768], P('fsdp')
- d_w_attn_out: float32 [768, 768], P('fsdp')
- d_b_attn_out: float32 [768], P('fsdp')
- d_ln1_gain: float32 [768], P('fsdp')
- d_ln1_bias: float32 [768], P('fsdp')
- d_w_inner: float32 [768, 3072], P('fsdp')
- d_b_inner: float32 [3072], P('fsdp')
- d_w_outer: float32 [3072, 768], P('fsdp')
- d_b_outer: float32 [768], P('fsdp')
- d_ln2_gain: float32 [768], P('fsdp')
- d_ln2_bias: float32 [768], P('fsdp')
- rms_values: float32 [3], replicated
Inputs may be any that keep to these rules, and one draw needn't show every extreme that they name: `segment_ids`: along a sequence the ids never fall; each id marks one document. `random_blocks`: block numbers of the same sequence, repeats allowed. `global_blocks`: block numbers of the same sequence, the two may coincide.
All inputs are finite; a program needn't handle non-finite values.
Results may differ from a plain program's by a relative error of at most 0.015.
Values may be sent and summed in bfloat16 or wider, within the bound.
A program may use at most 320 MiB of HBM per device.

v0:
```python
import jax
import jax.numpy as jnp
from jax import lax
from jax.sharding import PartitionSpec as P

HD = 64
BLK = 64


eps_norm = 1e-06


def layer_norm(hidden, gain_vec, shift_vec):
    mean_val = jnp.mean(hidden, axis=-1, keepdims=True)
    centred = hidden - mean_val
    var_val = jnp.mean(centred * centred, axis=-1, keepdims=True)
    return centred * lax.rsqrt(var_val + eps_norm) * gain_vec + shift_vec


def gelu_tanh(values):
    return jax.nn.gelu(values, approximate=True)


def contract_rows(left, right):
    return lax.dot_general(
        left, right, (((0,), (0,)), ((), ())), preferred_element_type=jnp.float32
    )


def times_transpose(left, right):
    return lax.dot_general(
        left, right, (((1,), (1,)), ((), ())), preferred_element_type=jnp.float32
    )


def allowed_mask(seg_row, rand_row, glob_row, start_at, span_len):
    full_len = seg_row.shape[0]
    block_ids = jnp.arange(full_len // BLK, dtype=jnp.int32)
    is_global = jnp.any(block_ids[:, None] == glob_row[None, :], axis=1)
    picked = jnp.any(rand_row[:, :, None] == block_ids[None, None, :], axis=1)
    nearby = jnp.abs(block_ids[:, None] - block_ids[None, :]) <= 1
    block_mask = nearby | picked | is_global[:, None] | is_global[None, :]
    block_rows = lax.dynamic_slice_in_dim(block_mask, start_at // BLK, span_len // BLK, 0)
    token_mask = jnp.repeat(jnp.repeat(block_rows, BLK, axis=0), BLK, axis=1)
    seg_query = lax.dynamic_slice_in_dim(seg_row, start_at, span_len, 0)
    return token_mask & (seg_query[:, None] == seg_row[None, :])


def attention_forward(q_heads, k_heads, v_heads, segment_ids, random_blocks, global_blocks):
    full_len = q_heads.shape[1]
    q_rows = min(512, full_len)
    block_count = full_len // q_rows
    score_scale = HD ** (-0.5)

    def per_row(packed):
        q_row, k_row, v_row, seg_row, rand_row, glob_row = packed

        def per_block(block_idx):
            start_at = block_idx * q_rows
            q_block = lax.dynamic_slice_in_dim(q_row, start_at, q_rows, 0)
            allowed = allowed_mask(seg_row, rand_row, glob_row, start_at, q_rows)
            scores = (
                jnp.einsum("qhd,khd->hqk", q_block, k_row, preferred_element_type=jnp.float32)
                * score_scale
            )
            scores = jnp.where(allowed[None], scores, -1e30)
            row_max = jnp.max(scores, axis=-1, keepdims=True)
            weights_raw = jnp.exp(scores - row_max)
            row_total = jnp.sum(weights_raw, axis=-1, keepdims=True)
            weights_low = (weights_raw / row_total).astype(jnp.bfloat16)
            attended = jnp.einsum(
                "hqk,khd->qhd", weights_low, v_row, preferred_element_type=jnp.float32
            ).astype(jnp.bfloat16)
            return (attended, (row_max + jnp.log(row_total))[:, :, 0])

        attended, log_sums = lax.map(per_block, jnp.arange(block_count, dtype=jnp.int32))
        return (attended.reshape(full_len, q_row.shape[1], q_row.shape[2]), log_sums)

    return lax.map(per_row, (q_heads, k_heads, v_heads, segment_ids, random_blocks, global_blocks))


def attention_backward(
    q_heads, k_heads, v_heads, grad_heads, log_sums, segment_ids, random_blocks, global_blocks
):
    full_len = q_heads.shape[1]
    q_rows = min(512, full_len)
    block_count = full_len // q_rows
    score_scale = HD ** (-0.5)

    def per_row(packed):
        q_row, k_row, v_row, grad_row, lse_row, seg_row, rand_row, glob_row = packed

        def step(carry, block_idx):
            dk_acc, dv_acc = carry
            start_at = block_idx * q_rows
            q_block = lax.dynamic_slice_in_dim(q_row, start_at, q_rows, 0)
            grad_block = lax.dynamic_slice_in_dim(grad_row, start_at, q_rows, 0)
            lse_block = lax.dynamic_index_in_dim(lse_row, block_idx, 0, keepdims=False)
            allowed = allowed_mask(seg_row, rand_row, glob_row, start_at, q_rows)
            scores = (
                jnp.einsum("qhd,khd->hqk", q_block, k_row, preferred_element_type=jnp.float32)
                * score_scale
            )
            scores = jnp.where(allowed[None], scores, -1e30)
            weights_full = jnp.exp(scores - lse_block[:, :, None])
            weights_low = weights_full.astype(jnp.bfloat16)
            dv_acc = dv_acc + jnp.einsum(
                "hqk,qhd->khd", weights_low, grad_block, preferred_element_type=jnp.float32
            )
            d_weights = jnp.einsum(
                "qhd,khd->hqk", grad_block, v_row, preferred_element_type=jnp.float32
            )
            d_scores = weights_full * (
                d_weights - jnp.sum(weights_full * d_weights, axis=-1, keepdims=True)
            )
            d_scores_low = d_scores.astype(jnp.bfloat16)
            dq_block = (
                jnp.einsum("hqk,khd->qhd", d_scores_low, k_row, preferred_element_type=jnp.float32)
                * score_scale
            )
            dk_acc = (
                dk_acc
                + jnp.einsum(
                    "hqk,qhd->khd", d_scores_low, q_block, preferred_element_type=jnp.float32
                )
                * score_scale
            )
            return ((dk_acc, dv_acc), dq_block.astype(jnp.bfloat16))

        zeros_kv = jnp.zeros(k_row.shape, jnp.float32)
        (dk_sum, dv_sum), dq_blocks = lax.scan(
            step, (zeros_kv, zeros_kv), jnp.arange(block_count, dtype=jnp.int32)
        )
        dq_row = dq_blocks.reshape(full_len, q_row.shape[1], q_row.shape[2])
        return (dq_row, dk_sum.astype(jnp.bfloat16), dv_sum.astype(jnp.bfloat16))

    return lax.map(
        per_row,
        (
            q_heads,
            k_heads,
            v_heads,
            grad_heads,
            log_sums,
            segment_ids,
            random_blocks,
            global_blocks,
        ),
    )


def shards(
    tokens_in,
    segment_ids,
    random_blocks,
    global_blocks,
    w_query,
    b_query,
    w_key,
    w_value,
    b_value,
    w_attn_out,
    b_attn_out,
    ln1_gain,
    ln1_bias,
    w_inner,
    b_inner,
    w_outer,
    b_outer,
    ln2_gain,
    ln2_bias,
    out_grad,
):
    row_count, local_len, model_width = tokens_in.shape
    seq_count = lax.axis_size("seq")
    fsdp_count = lax.axis_size("fsdp")
    tok_count = row_count * local_len
    head_group = model_width // seq_count
    heads_here = head_group // HD
    full_len = local_len * seq_count
    flat_in = tokens_in.reshape(tok_count, model_width)

    def to_groups(values):
        return values.reshape(row_count, local_len, seq_count, head_group)

    def to_heads(values):
        return values.reshape(row_count, full_len, heads_here, HD)

    def from_heads(values):
        return values.reshape(row_count, full_len, 1, head_group)

    query_w, key_w, value_w, out_w, query_b, value_b, out_b, gain_one, bias_one = (
        lax.all_gather(w_query, "fsdp", axis=0, tiled=True),
        lax.all_gather(w_key, "fsdp", axis=0, tiled=True),
        lax.all_gather(w_value, "fsdp", axis=0, tiled=True),
        lax.all_gather(w_attn_out, "fsdp", axis=0, tiled=True),
        lax.all_gather(b_query, "fsdp", axis=0, tiled=True),
        lax.all_gather(b_value, "fsdp", axis=0, tiled=True),
        lax.all_gather(b_attn_out, "fsdp", axis=0, tiled=True),
        lax.all_gather(ln1_gain, "fsdp", axis=0, tiled=True),
        lax.all_gather(ln1_bias, "fsdp", axis=0, tiled=True),
    )
    queries = (jnp.dot(flat_in, query_w, preferred_element_type=jnp.float32) + query_b).astype(
        jnp.bfloat16
    )
    keys_proj = jnp.dot(flat_in, key_w, preferred_element_type=jnp.float32).astype(jnp.bfloat16)
    values_proj = (jnp.dot(flat_in, value_w, preferred_element_type=jnp.float32) + value_b).astype(
        jnp.bfloat16
    )
    q_group, k_group, v_group = (
        lax.all_to_all(to_groups(queries), "seq", split_axis=2, concat_axis=1, tiled=True),
        lax.all_to_all(to_groups(keys_proj), "seq", split_axis=2, concat_axis=1, tiled=True),
        lax.all_to_all(to_groups(values_proj), "seq", split_axis=2, concat_axis=1, tiled=True),
    )
    q_heads = to_heads(q_group)
    k_heads = to_heads(k_group)
    v_heads = to_heads(v_group)
    att_heads, log_sums = attention_forward(
        q_heads, k_heads, v_heads, segment_ids, random_blocks, global_blocks
    )
    att_local = lax.all_to_all(
        from_heads(att_heads), "seq", split_axis=1, concat_axis=2, tiled=True
    )
    att_flat = att_local.reshape(tok_count, model_width)
    attn_branch = jnp.dot(att_flat, out_w, preferred_element_type=jnp.float32) + out_b
    resid_one = flat_in.astype(jnp.float32) + attn_branch
    normed_one, norm_one_pull = jax.vjp(
        layer_norm, resid_one, gain_one.astype(jnp.float32), bias_one.astype(jnp.float32)
    )
    normed_low = normed_one.astype(jnp.bfloat16)
    inner_w, outer_w, inner_b, outer_b, gain_two, bias_two = (
        lax.all_gather(w_inner, "fsdp", axis=0, tiled=True),
        lax.all_gather(w_outer, "fsdp", axis=0, tiled=True),
        lax.all_gather(b_inner, "fsdp", axis=0, tiled=True),
        lax.all_gather(b_outer, "fsdp", axis=0, tiled=True),
        lax.all_gather(ln2_gain, "fsdp", axis=0, tiled=True),
        lax.all_gather(ln2_bias, "fsdp", axis=0, tiled=True),
    )
    inner_pre = jnp.dot(normed_low, inner_w, preferred_element_type=jnp.float32) + inner_b
    inner_act, gelu_pull = jax.vjp(gelu_tanh, inner_pre)
    inner_low = inner_act.astype(jnp.bfloat16)
    mlp_branch = jnp.dot(inner_low, outer_w, preferred_element_type=jnp.float32) + outer_b
    normed_two, norm_two_pull = jax.vjp(
        layer_norm,
        normed_one + mlp_branch,
        gain_two.astype(jnp.float32),
        bias_two.astype(jnp.float32),
    )
    stream_sums = lax.psum(
        (
            jnp.sum(resid_one * resid_one),
            jnp.sum(attn_branch * attn_branch),
            jnp.sum(mlp_branch * mlp_branch),
        ),
        ("seq", "fsdp"),
    )
    entry_total = tok_count * model_width * seq_count * fsdp_count
    rms_values = jnp.sqrt(jnp.stack([stream_sums[0], stream_sums[1], stream_sums[2]]) / entry_total)
    inner_w, outer_w = (
        lax.all_gather(w_inner, "fsdp", axis=0, tiled=True),
        lax.all_gather(w_outer, "fsdp", axis=0, tiled=True),
    )
    d_resid_two, d_gain_two, d_bias_two = norm_two_pull(
        out_grad.reshape(tok_count, model_width).astype(jnp.float32)
    )
    d_mlp = d_resid_two.astype(jnp.bfloat16)
    d_outer_b = jnp.sum(d_mlp.astype(jnp.float32), axis=0)
    d_outer_w = contract_rows(inner_low, d_mlp)
    (d_pre_full,) = gelu_pull(times_transpose(d_mlp, outer_w))
    d_pre = d_pre_full.astype(jnp.bfloat16)
    d_inner_b = jnp.sum(d_pre.astype(jnp.float32), axis=0)
    d_inner_w = contract_rows(normed_low, d_pre)
    d_normed_one = d_resid_two + times_transpose(d_pre, inner_w)
    d_resid_one, d_gain_one, d_bias_one = norm_one_pull(d_normed_one)
    query_w, key_w, value_w, out_w = (
        lax.all_gather(w_query, "fsdp", axis=0, tiled=True),
        lax.all_gather(w_key, "fsdp", axis=0, tiled=True),
        lax.all_gather(w_value, "fsdp", axis=0, tiled=True),
        lax.all_gather(w_attn_out, "fsdp", axis=0, tiled=True),
    )
    d_attn = d_resid_one.astype(jnp.bfloat16)
    d_out_b = jnp.sum(d_attn.astype(jnp.float32), axis=0)
    d_out_w = contract_rows(att_flat, d_attn)
    d_att = times_transpose(d_attn, out_w).astype(jnp.bfloat16)
    grad_group = lax.all_to_all(to_groups(d_att), "seq", split_axis=2, concat_axis=1, tiled=True)
    dq_heads, dk_heads, dv_heads = attention_backward(
        q_heads,
        k_heads,
        v_heads,
        to_heads(grad_group),
        log_sums,
        segment_ids,
        random_blocks,
        global_blocks,
    )
    dq_local, dk_local, dv_local = (
        lax.all_to_all(from_heads(dq_heads), "seq", split_axis=1, concat_axis=2, tiled=True),
        lax.all_to_all(from_heads(dk_heads), "seq", split_axis=1, concat_axis=2, tiled=True),
        lax.all_to_all(from_heads(dv_heads), "seq", split_axis=1, concat_axis=2, tiled=True),
    )
    dq_flat = dq_local.reshape(tok_count, model_width)
    dk_flat = dk_local.reshape(tok_count, model_width)
    dv_flat = dv_local.reshape(tok_count, model_width)
    d_query_b = jnp.sum(dq_flat.astype(jnp.float32), axis=0)
    d_value_b = jnp.sum(dv_flat.astype(jnp.float32), axis=0)
    d_query_w = contract_rows(flat_in, dq_flat)
    d_key_w = contract_rows(flat_in, dk_flat)
    d_value_w = contract_rows(flat_in, dv_flat)
    d_tokens = (
        d_resid_one
        + times_transpose(dq_flat, query_w)
        + times_transpose(dk_flat, key_w)
        + times_transpose(dv_flat, value_w)
    )
    shard_list = (
        lax.psum_scatter(d_query_w, "fsdp", scatter_dimension=0, tiled=True),
        lax.psum_scatter(d_query_b, "fsdp", scatter_dimension=0, tiled=True),
        lax.psum_scatter(d_key_w, "fsdp", scatter_dimension=0, tiled=True),
        lax.psum_scatter(d_value_w, "fsdp", scatter_dimension=0, tiled=True),
        lax.psum_scatter(d_value_b, "fsdp", scatter_dimension=0, tiled=True),
        lax.psum_scatter(d_out_w, "fsdp", scatter_dimension=0, tiled=True),
        lax.psum_scatter(d_out_b, "fsdp", scatter_dimension=0, tiled=True),
        lax.psum_scatter(d_gain_one, "fsdp", scatter_dimension=0, tiled=True),
        lax.psum_scatter(d_bias_one, "fsdp", scatter_dimension=0, tiled=True),
        lax.psum_scatter(d_inner_w, "fsdp", scatter_dimension=0, tiled=True),
        lax.psum_scatter(d_inner_b, "fsdp", scatter_dimension=0, tiled=True),
        lax.psum_scatter(d_outer_w, "fsdp", scatter_dimension=0, tiled=True),
        lax.psum_scatter(d_outer_b, "fsdp", scatter_dimension=0, tiled=True),
        lax.psum_scatter(d_gain_two, "fsdp", scatter_dimension=0, tiled=True),
        lax.psum_scatter(d_bias_two, "fsdp", scatter_dimension=0, tiled=True),
    )
    (
        s_query_w,
        s_query_b,
        s_key_w,
        s_value_w,
        s_value_b,
        s_out_w,
        s_out_b,
        s_gain_one,
        s_bias_one,
        s_inner_w,
        s_inner_b,
        s_outer_w,
        s_outer_b,
        s_gain_two,
        s_bias_two,
    ) = shard_list
    summed = (
        lax.psum(s_query_w.astype(jnp.bfloat16), "seq").astype(jnp.float32),
        lax.psum(s_query_b.astype(jnp.bfloat16), "seq").astype(jnp.float32),
        lax.psum(s_key_w.astype(jnp.bfloat16), "seq").astype(jnp.float32),
        lax.psum(s_value_w.astype(jnp.bfloat16), "seq").astype(jnp.float32),
        lax.psum(s_value_b.astype(jnp.bfloat16), "seq").astype(jnp.float32),
        lax.psum(s_out_w.astype(jnp.bfloat16), "seq").astype(jnp.float32),
        lax.psum(s_out_b.astype(jnp.bfloat16), "seq").astype(jnp.float32),
        lax.psum(s_gain_one.astype(jnp.bfloat16), "seq").astype(jnp.float32),
        lax.psum(s_bias_one.astype(jnp.bfloat16), "seq").astype(jnp.float32),
        lax.psum(s_inner_w.astype(jnp.bfloat16), "seq").astype(jnp.float32),
        lax.psum(s_inner_b.astype(jnp.bfloat16), "seq").astype(jnp.float32),
        lax.psum(s_outer_w.astype(jnp.bfloat16), "seq").astype(jnp.float32),
        lax.psum(s_outer_b.astype(jnp.bfloat16), "seq").astype(jnp.float32),
        lax.psum(s_gain_two.astype(jnp.bfloat16), "seq").astype(jnp.float32),
        lax.psum(s_bias_two.astype(jnp.bfloat16), "seq").astype(jnp.float32),
    )
    out_tokens = normed_two.astype(jnp.bfloat16).reshape(row_count, local_len, model_width)
    d_tokens_in = d_tokens.astype(jnp.bfloat16).reshape(row_count, local_len, model_width)
    return (
        out_tokens,
        d_tokens_in,
        summed[0],
        summed[1],
        summed[2],
        summed[3],
        summed[4],
        summed[5],
        summed[6],
        summed[7],
        summed[8],
        summed[9],
        summed[10],
        summed[11],
        summed[12],
        summed[13],
        summed[14],
        rms_values,
    )


def solution(mesh):
    in_specs = (
        P("fsdp", "seq", None),
        P("fsdp", None),
        P("fsdp", None, None),
        P("fsdp", None),
        P("fsdp", None),
        P("fsdp"),
        P("fsdp", None),
        P("fsdp", None),
        P("fsdp"),
        P("fsdp", None),
        P("fsdp"),
        P("fsdp"),
        P("fsdp"),
        P("fsdp", None),
        P("fsdp"),
        P("fsdp", None),
        P("fsdp"),
        P("fsdp"),
        P("fsdp"),
        P("fsdp", "seq", None),
    )
    out_specs = (
        P("fsdp", "seq", None),
        P("fsdp", "seq", None),
        P("fsdp", None),
        P("fsdp"),
        P("fsdp", None),
        P("fsdp", None),
        P("fsdp"),
        P("fsdp", None),
        P("fsdp"),
        P("fsdp"),
        P("fsdp"),
        P("fsdp", None),
        P("fsdp"),
        P("fsdp", None),
        P("fsdp"),
        P("fsdp"),
        P("fsdp"),
        P(),
    )
    return jax.shard_map(shards, mesh=mesh, in_specs=in_specs, out_specs=out_specs, check_vma=False)
```

profile of v0, /device:TPU:0, one launch (start us, length us, event | category | flops | bytes accessed | tf_op | source)
XLA Modules:
  0.0 2195.0 jit_solution(13270577368292568597)
XLA Ops:
  20.8 63.2 %all-reduce.20 = (bf16[768]{0:T(1024)(128)(2,1)S(1)}, bf16[768]{0:T(1024)(128)(2,1)S(1)}, bf16[768]{0:T(1024)(128)(2,1)}, bf16[768]{0:T(1024)(128)(2,1)}, bf16[7...) all-reduce(bf16[768]{0:T(1024)(128)(2,1)S(1)} %dynamic-update-slice, ...), channel_id=1, replica_groups=mesh['seq'=2,'fsdp'=16] {'fsdp'}, use_global_device_ids=true, to_apply=%add | all-reduce | flops 9216 | bytes 36864
  120.0 14.4 all-to-all-done
  157.3 13.8 all-to-all-done.2
  220.2 381.0 %while.85 = (s32[]{:T(128)}, bf16[2,2048,6,64]{1,3,2,0:T(8,128)(2,1)}, f32[2,4,6,512]{3,2,1,0:T(8,128)}, bf16[2,2048,6,64]{1,3,2,0:T(8,128)(2,1)}, s32[2,2]{1,0:...) while((s32[]{:T(128)}, ...), condition=%wide.region_7.8_spmd, body=%wide.region_0.7_spmd.sunk | while | flops 1688407936 | bytes 111215376 | solution.py:79
  228.4 171.1 %while.88 = (s32[]{:T(128)}, bf16[4,512,6,64]{1,3,2,0:T(8,128)(2,1)}, f32[4,6,512]{2,1,0:T(8,128)S(1)}, s32[32,3]{0,1:T(4,128)S(1)}, s32[2]{0:T(128)S(1)}, /*ind...) while((s32[]{:T(128)}, ...), condition=%wide.region_6.6_spmd, body=%wide.region_1.5_spmd.sunk | while | flops 1688407936 | bytes 92207768 | solution.py:76
  419.3 170.4 %while.88 = (s32[]{:T(128)}, bf16[4,512,6,64]{1,3,2,0:T(8,128)(2,1)}, f32[4,6,512]{2,1,0:T(8,128)S(1)}, s32[32,3]{0,1:T(4,128)S(1)}, s32[2]{0:T(128)S(1)}, /*ind...) while((s32[]{:T(128)}, ...), condition=%wide.region_6.6_spmd, body=%wide.region_1.5_spmd.sunk | while | flops 1688407936 | bytes 92207768 | solution.py:76
  614.4 29.5 %all-to-all-done.3 = bf16[2,2048,1,384]{3,0,2,1:T(2,128)(2,1)S(1)} async-done(((bf16[2,2048,1,384]{3,0,2,1:T(2,128)(2,1)}), bf16[2,2048,1,384]{3,0,2,1:T(2,128)(2,1)S(1)}, u32[]{:S(2)}, u32[]{:S(2)}) %all-to-all-start.3) | async-done | bytes 3145760 | tf_op jit(solution)/shard_map/all_to_all | solution.py:221
  659.1 23.9 %multiply_convert_fusion.1 = (bf16[2048,3072]{1,0:T(8,128)(2,1)}, f32[2048,3072]{1,0:T(8,128)}) fusion(f32[3072]{0:T(1024)S(1)} %convert_element_type.237, bf16[768,3072]{1,0:T(8,128)(2,1)} %all-gather.15.cloned.1.call-done, f32[2048,768]{1,0:T(8,128)} %copy-done.7, f32[768]{0:T(1024)S(1)} %convert_element_type.235, f32[768]{0:T(1024)S(1)} %convert_element_type.234, ...), kind=kOutput, calls=%fused_computation.92 | convolution fusion | flops 9734455296 | bytes 48793600 | tf_op jit(solution)/shard_map/dot_general | solution.py:239
  683.0 17.0 fusion.68
  712.8 31.1 %convert_reduce_fusion = (f32[3072]{0:T(1024)}, bf16[2048,3072]{1,0:T(8,128)(2,1)}) fusion(f32[2048,3072]{1,0:T(8,128)} %get-tuple-element.1098, f32[3072]{0:T(1024)S(1)} %convert_element_type.237, bf16[2048,768]{1,0:T(8,128)(2,1)S(1)} %get-tuple-element.1073, bf16[3072,768]{1,0:T(8,128)(2,1)} %all-gather.17.cloned.1.call-done), kind=kOutput, calls=%fused_computation.91 | convolution fusion | flops 9808376832 | bytes 45637632 | tf_op jit(solution)/shard_map/dot_general | solution.py:31
  744.0 19.4 multiply_reduce_fusion.4
  795.1 21.6 all-to-all-done.4
  834.9 788.1 %while.87 = (s32[]{:T(128)}, bf16[2,2048,6,64]{1,3,2,0:T(8,128)(2,1)}, bf16[2,2048,6,64]{1,3,2,0:T(8,128)(2,1)}, bf16[2,2048,6,64]{1,3,2,0:T(8,128)(2,1)}, bf16[...) while((s32[]{:T(128)}, ...), condition=%wide.region_22.23_spmd, body=%wide.region_16.22_spmd.sunk | while | flops 4128903168 | bytes 264922096 | solution.py:137
  849.2 365.2 %while.89 = (s32[]{:T(128)}, f32[2048,6,64]{0,2,1:T(8,128)}, f32[2048,6,64]{0,2,1:T(8,128)}, bf16[4,512,6,64]{1,3,2,0:T(8,128)(2,1)}, s32[4]{0:T(128)S(1)}, /*in...) while((s32[]{:T(128)}, f32[2048,6,64]{0,2,1:T(8,128)}, ...), condition=%wide.region_21.21_spmd.clone, body=%wide.region_17.20_spmd.clone.sunk | while | flops 4127330304 | bytes 227056384 | solution.py:131
  854.2 13.6 fusion.151
  869.8 17.5 multiply_reduce_fusion.9
  887.2 21.3 multiply_convert_fusion.3
  959.7 17.4 multiply_reduce_fusion.9
  977.1 21.3 multiply_convert_fusion.3
  1017.3 13.7 bitcast_add_fusion.5
  1051.4 17.4 multiply_reduce_fusion.9
  1068.8 21.3 multiply_convert_fusion.3
  1109.0 13.7 bitcast_add_fusion.5
  1143.1 17.4 multiply_reduce_fusion.9
  1160.5 21.3 multiply_convert_fusion.3
  1200.7 13.7 bitcast_add_fusion.5
  1243.1 364.9 %while.89 = (s32[]{:T(128)}, f32[2048,6,64]{0,2,1:T(8,128)}, f32[2048,6,64]{0,2,1:T(8,128)}, bf16[4,512,6,64]{1,3,2,0:T(8,128)(2,1)}, s32[4]{0:T(128)S(1)}, /*in...) while((s32[]{:T(128)}, f32[2048,6,64]{0,2,1:T(8,128)}, ...), condition=%wide.region_21.21_spmd.clone, body=%wide.region_17.20_spmd.clone.sunk | while | flops 4127330304 | bytes 227056384 | solution.py:131
  1263.5 17.4 multiply_reduce_fusion.9
  1280.9 21.3 multiply_convert_fusion.3
  1353.4 17.4 multiply_reduce_fusion.9
  1370.8 21.3 multiply_convert_fusion.3
  1411.0 13.7 bitcast_add_fusion.5
  1445.1 17.4 multiply_reduce_fusion.9
  1462.5 21.3 multiply_convert_fusion.3
  1502.7 13.7 bitcast_add_fusion.5
  1536.8 17.4 multiply_reduce_fusion.9
  1554.2 21.3 multiply_convert_fusion.3
  1594.4 13.7 bitcast_add_fusion.5
  1631.3 30.6 %all_to_all.120 = bf16[2,2048,1,384]{3,0,2,1:T(2,128)(2,1)S(1)} all-to-all(bf16[2,2048,1,384]{3,0,2,1:T(2,128)(2,1)S(1)} %copy.210), channel_id=1, replica_groups=mesh['seq'=2,'fsdp'=16] {'seq'}, dimensions={1} | all-to-all | bytes 6291456 | tf_op jit(solution)/shard_map/all_to_all | solution.py:298
  1681.2 30.9 %all_to_all.121 = bf16[2,2048,1,384]{3,0,2,1:T(2,128)(2,1)S(1)} all-to-all(bf16[2,2048,1,384]{3,0,2,1:T(2,128)(2,1)} %copy.213), channel_id=1, replica_groups=mesh['seq'=2,'fsdp'=16] {'seq'}, dimensions={1} | all-to-all | bytes 6291456 | tf_op jit(solution)/shard_map/all_to_all | solution.py:299
  1734.7 30.0 %all_to_all.122 = bf16[2,2048,1,384]{3,0,2,1:T(2,128)(2,1)S(1)} all-to-all(bf16[2,2048,1,384]{3,0,2,1:T(2,128)(2,1)} %copy.208), channel_id=1, replica_groups=mesh['seq'=2,'fsdp'=16] {'seq'}, dimensions={1} | all-to-all | bytes 6291456 | tf_op jit(solution)/shard_map/all_to_all | solution.py:297
  1777.8 18.9 fusion.62
  1796.8 16.3 fusion.74
  1816.9 79.3 %all-reduce.18 = (f32[1]{0:T(128)}, f32[1]{0:T(128)}, f32[1]{0:T(128)}) all-reduce(f32[1]{0:T(128)} %bitcast.56, f32[1]{0:T(128)} %bitcast.55, f32[1]{0:T(128)} %bitcast.54), channel_id=1, replica_groups=mesh['seq'=2,'fsdp'=16] {'seq','fsdp'}, use_global_device_ids=true, to_apply=%region_67.68 | all-reduce | flops 3 | bytes 24 | tf_op jit(solution)/shard_map/psum | solution.py:249
  1904.5 62.4 %all-reduce.19 = (bf16[768]{0:T(1024)(128)(2,1)S(1)}, bf16[768]{0:T(1024)(128)(2,1)S(1)}, bf16[768]{0:T(1024)(128)(2,1)S(1)}, bf16[768]{0:T(1024)(128)(2,1)S(1)}...) all-reduce(f32[768]{0:T(1024)S(1)} %reduce_sum.249, ...), channel_id=3, replica_groups=mesh['seq'=2,'fsdp'=16] {'fsdp'}, use_global_device_ids=true, to_apply=%region_26.27.clone | all-reduce | flops 9216 | bytes 55296
  1996.2 17.2 reduce-scatter.15.cloned.1.call-done
  2015.2 113.8 %reduce-scatter.17.cloned.1.call-done = f32[192,768]{1,0:T(8,128)} async-done(((f32[3072,768]{1,0:T(8,128)}), f32[192,768]{1,0:T(8,128)}) %reduce-scatter.17.cloned.1.call-update) | async-done | bytes 589840 | tf_op jit(solution)/shard_map/reduce_scatter | solution.py:327
  2140.3 37.7 %all-reduce.25.cloned.1.call-done = (bf16[48,768]{0,1:T(8,128)(2,1)}, bf16[48,768]{0,1:T(8,128)(2,1)}, bf16[48,768]{0,1:T(8,128)(2,1)}, bf16[48,768]{1,0:T(8,128...) async-done(((bf16[48,768]{0,1:T(8,128)(2,1)}, bf16[48,768]{0,1:T(8,128)(2,1)}, bf16[48,768]{0,1:T(8,128)(2,1)}, bf16[48,768]{1,0:T(8,128)(2,1)}, ...) | async-done | bytes 884752 | tf_op jit(solution)/shard_map/psum | solution.py:350
  (613 shorter events, 1073.3 us)
Async XLA Ops:
  7.2 76.7 %all-gather.7.cloned.1.call-start = ((), (), s32[]{:S(2)}) async-start(), calls=%async_computation.14 | async-start | bytes 1253376 | tf_op jit(solution)/shard_map/all_gather | solution.py:193
  7.9 94.4 %all-gather.11.cloned.1.call-start = ((), (), s32[]{:S(2)}) async-start(), calls=%async_computation.16 | async-start | bytes 1253376 | tf_op jit(solution)/shard_map/all_gather | solution.py:195
  8.7 131.2 %all-gather.9.cloned.1.call-start = ((), (), s32[]{:S(2)}) async-start(), calls=%async_computation.15 | async-start | bytes 1253376 | tf_op jit(solution)/shard_map/all_gather | solution.py:194
  9.4 638.4 %all-gather.13.cloned.1.call-start = ((), (), s32[]{:S(2)}) async-start(), calls=%async_computation.17 | async-start | bytes 1253376 | tf_op jit(solution)/shard_map/all_gather | solution.py:196
  10.0 649.1 %all-gather.15.cloned.1.call-start = ((), (), s32[]{:S(2)}) async-start(), calls=%async_computation.18 | async-start | bytes 5013504 | tf_op jit(solution)/shard_map/all_gather | solution.py:232
  98.4 36.0 %all-to-all-start = ((bf16[2,1024,2,384]{3,1,0,2:T(8,128)(2,1)}), bf16[2,1024,2,384]{3,1,0,2:T(8,128)(2,1)S(1)}, u32[]{:S(2)}, u32[]{:S(2)}) async-start(bf16[2,1024,2,384]{3,1,0,2:T(8,128)(2,1)} %copy.192), calls=%async_computation | async-start | bytes 6291456 | tf_op jit(solution)/shard_map/all_to_all | solution.py:211
  134.3 36.8 %all-to-all-start.2 = ((bf16[2,1024,2,384]{3,1,0,2:T(8,128)(2,1)}), bf16[2,1024,2,384]{3,1,0,2:T(8,128)(2,1)}, u32[]{:S(2)}, u32[]{:S(2)}) async-start(bf16[2,1024,2,384]{3,1,0,2:T(8,128)(2,1)} %copy.196), calls=%async_computation.2 | async-start | bytes 6291456 | tf_op jit(solution)/shard_map/all_to_all | solution.py:213
  157.3 19.7 copy-start.35
  171.1 35.7 %all-to-all-start.1 = ((bf16[2,1024,2,384]{3,1,0,2:T(8,128)(2,1)}), bf16[2,1024,2,384]{3,1,0,2:T(8,128)(2,1)}, u32[]{:S(2)}, u32[]{:S(2)}) async-start(bf16[2,1024,2,384]{3,1,0,2:T(8,128)(2,1)} %copy.194), calls=%async_computation.1 | async-start | bytes 6291456 | tf_op jit(solution)/shard_map/all_to_all | solution.py:212
  176.5 506.6 %all-gather.17.cloned.1.call-start = ((), (), s32[]{:S(2)}) async-start(), calls=%async_computation.19 | async-start | bytes 5013504 | tf_op jit(solution)/shard_map/all_gather | solution.py:233
  246.8 12.6 copy-start.2
  290.0 12.1 copy-start.2
  332.6 12.1 copy-start.2
  375.2 12.1 copy-start.2
  437.6 12.1 copy-start.2
  480.1 12.1 copy-start.2
  610.1 33.7 %all-to-all-start.3 = ((bf16[2,2048,1,384]{3,0,2,1:T(2,128)(2,1)}), bf16[2,2048,1,384]{3,0,2,1:T(2,128)(2,1)S(1)}, u32[]{:S(2)}, u32[]{:S(2)}) async-start(bf16[2,2048,1,384]{3,0,2,1:T(2,128)(2,1)} %copy.200), calls=%async_computation.3 | async-start | bytes 6291456 | tf_op jit(solution)/shard_map/all_to_all | solution.py:221
  614.3 149.1 %copy-start.27 = (f32[768]{0:T(1024)}, f32[768]{0:T(1024)S(1)}, u32[]{:S(2)}) copy-start(f32[768]{0:T(1024)S(1)} %convert_element_type.234) | copy-start | bytes 9220
  614.3 68.7 %copy-start.31 = (f32[768]{0:T(1024)}, f32[768]{0:T(1024)S(1)}, u32[]{:S(2)}) copy-start(f32[768]{0:T(1024)S(1)} %convert_element_type.235) | copy-start | bytes 9220
  655.5 107.9 %copy-start.18 = (f32[2048]{0:T(1024)}, f32[2048]{0:T(1024)S(1)}, u32[]{:S(2)}) copy-start(f32[2048]{0:T(1024)S(1)} %broadcast_multiply_fusion.1) | copy-start | bytes 24580
  659.0 104.4 %copy-start.22 = (f32[2048]{0:T(1024)}, f32[2048]{0:T(1024)S(1)}, u32[]{:S(2)}) copy-start(f32[2048]{0:T(1024)S(1)} %fusion.59) | copy-start | bytes 24580
  709.6 34.3 %slice-start = ((s8[6291456]{0:T(1024)(128)(4,1)}), s8[4194304]{0:T(1024)(128)(4,1)S(1)}, s32[]{:S(2)}) async-start(s8[6291456]{0:T(1024)(128)(4,1)} %bitcast.264), calls=%async_computation.27 | async-start | bytes 8388608
  712.8 31.1 %copy-start.10 = (bf16[2048,768]{1,0:T(8,128)(2,1)}, bf16[2048,768]{1,0:T(8,128)(2,1)S(1)}, u32[]{:S(2)}) copy-start(bf16[2048,768]{1,0:T(8,128)(2,1)S(1)} %get-tuple-element.1073) | copy-start | bytes 9437188
  712.8 31.1 %slice-start.1 = ((s8[6291456]{0:T(1024)(128)(4,1)}), s8[2097152]{0:T(1024)(128)(4,1)S(1)}, s32[]{:S(2)}) async-start(s8[6291456]{0:T(1024)(128)(4,1)} %bitcast.264), calls=%async_computation.28 | async-start | bytes 4194304
  784.0 32.7 %all-to-all-start.4 = ((bf16[2,1024,2,384]{3,1,0,2:T(8,128)(2,1)}), bf16[2,1024,2,384]{3,1,0,2:T(8,128)(2,1)S(1)}, u32[]{:S(2)}, u32[]{:S(2)}) async-start(bf16[2,1024,2,384]{3,1,0,2:T(8,128)(2,1)} %copy.202), calls=%async_computation.4 | async-start | bytes 6291456 | tf_op jit(solution)/shard_map/all_to_all | solution.py:285
  788.0 1201.4 %reduce-scatter.13.cloned.1.call-start = ((), (), s32[]{:S(2)}) async-start(), calls=%async_computation.20 | async-start | bytes 2506752 | tf_op jit(solution)/shard_map/reduce_scatter | solution.py:321
  795.0 1196.0 %reduce-scatter.21.cloned.1.call-start = ((), (), s32[]{:S(2)}) async-start(), calls=%async_computation.24 | async-start | bytes 2506752
  854.2 15.5 copy-start.1
  944.3 15.4 copy-start.1
  1036.0 15.4 copy-start.1
  1127.7 15.4 copy-start.1
  1248.1 15.4 copy-start.1
  1338.0 15.4 copy-start.1
  1429.7 15.4 copy-start.1
  1521.4 15.4 copy-start.1
  1675.4 317.3 %reduce-scatter.23.cloned.1.call-start = ((), (), s32[]{:S(2)}) async-start(), calls=%async_computation.25 | async-start | bytes 2506752
  1725.8 268.6 %reduce-scatter.19.cloned.1.call-start = ((), (), s32[]{:S(2)}) async-start(), calls=%async_computation.23 | async-start | bytes 2506752
  1777.7 235.7 %reduce-scatter.15.cloned.1.call-start = ((), (), s32[]{:S(2)}) async-start(), calls=%async_computation.21 | async-start | bytes 10027008 | tf_op jit(solution)/shard_map/reduce_scatter | solution.py:325
  1796.7 332.3 %reduce-scatter.17.cloned.1.call-start = ((), (), s32[]{:S(2)}) async-start(), calls=%async_computation.22 | async-start | bytes 10027008 | tf_op jit(solution)/shard_map/reduce_scatter | solution.py:327
  1813.1 364.9 %all-reduce.25.cloned.1.call-start = ((), (), s32[]{:S(2)}) async-start(), calls=%async_computation.26 | async-start | bytes 2506752 | tf_op jit(solution)/shard_map/psum | solution.py:350
  1814.4 90.0 %copy-start.24 = (f32[768]{0:T(1024)S(1)}, f32[768]{0:T(1024)}, u32[]{:S(2)}) copy-start(f32[768]{0:T(1024)} %get-tuple-element.1072) | copy-start | bytes 9220
  1814.5 90.0 %copy-start.25 = (f32[768]{0:T(1024)S(1)}, f32[768]{0:T(1024)}, u32[]{:S(2)}) copy-start(f32[768]{0:T(1024)} %get-tuple-element.1074) | copy-start | bytes 9220
  1814.5 90.0 %copy-start.26 = (f32[768]{0:T(1024)S(1)}, f32[768]{0:T(1024)}, u32[]{:S(2)}) copy-start(f32[768]{0:T(1024)} %get-tuple-element.944) | copy-start | bytes 9220
  1814.5 90.0 %copy-start.29 = (f32[3072]{0:T(1024)S(1)}, f32[3072]{0:T(1024)}, u32[]{:S(2)}) copy-start(f32[3072]{0:T(1024)} %get-tuple-element.1100) | copy-start | bytes 36868
  1814.5 90.0 %copy-start.33 = (f32[768]{0:T(1024)S(1)}, f32[768]{0:T(1024)}, u32[]{:S(2)}) copy-start(f32[768]{0:T(1024)} %get-tuple-element.942) | copy-start | bytes 9220
  1814.5 90.0 %copy-start.34 = (f32[768]{0:T(1024)S(1)}, f32[768]{0:T(1024)}, u32[]{:S(2)}) copy-start(f32[768]{0:T(1024)} %get-tuple-element.947) | copy-start | bytes 9220
  1984.8 146.1 %copy-start.13 = (bf16[256,8,2,384]{3,1,2,0:T(8,128)(2,1)S(1)}, bf16[256,8,2,384]{3,1,2,0:T(8,128)(2,1)}, u32[]{:S(2)}) copy-start(bf16[256,8,2,384]{3,1,2,0:T(8,128)(2,1)} %copy-done.12) | copy-start | bytes 9437188
  1984.8 146.1 %copy-start.21 = (f32[2048]{0:T(1024)S(1)}, f32[2048]{0:T(1024)}, u32[]{:S(2)}) copy-start(f32[2048]{0:T(1024)} %copy-done.20) | copy-start | bytes 24580
  (41 other events, 213.9 us)
Sparse Core Ops, SparseCore 0:
  10.3 41.1 all-gather.6
  53.8 37.2 all-gather.10
  93.3 37.4 all-gather.8
  133.0 37.2 all-gather.12
  172.4 52.2 all-gather.14
  226.8 51.9 all-gather.16
  795.1 80.3 reduce-scatter.12
  1675.5 90.9 reduce-scatter.20
  1770.3 61.9 reduce-scatter.22
  1836.4 62.2 reduce-scatter.18
  1902.7 110.6 reduce-scatter.14
  2017.9 111.0 reduce-scatter.16
  2132.8 45.1 all-reduce.24
where the time goes:
time: 2210 us; the launch traced here: 2200 us
  matrix products  893 us (40%)
  other arithmetic  343 us (16%)
  local copies, waits for them, and re-layouts  330 us (15%)
  blocking collectives  301 us (14%)
  waiting for transfers between devices  258 us (12%)
  loops' own time  28.1 us (1%)
  starting transfers between devices  23.4 us (1%)
    convert_element_type x8, other arithmetic, step(): d_scores_low = d_scores.astype(jnp.bfloat16)  170 us
    dot_general x8, matrix products, step(): jnp.einsum('qhd,khd->hqk', grad_block, v_row, preferred_element_type=jnp....  139 us
    unnamed x2, blocking collectives  126 us
    reduce_scatter x1, waiting for transfers between devices, shards(): lax.psum_scatter(d_outer_w, 'fsdp', scatter_dimension=0, tiled=True)  114 us
    dot_general x8, matrix products, step(): jnp.einsum('hqk,qhd->khd', weights_low, grad_block, preferred_element_typ...  108 us
    dot_general x8, matrix products, step(): jnp.einsum('qhd,khd->hqk', q_block, k_row, preferred_element_type=jnp.flo...  107 us
    dot_general x8, matrix products, per_block(): jnp.einsum('hqk,khd->qhd', weights_low, v_row, preferred_element_type=jnp...  98.4 us
    reduce_sum x8, other arithmetic, per_block(): row_total = jnp.sum(weights_raw, axis=-1, keepdims=True)  96.8 us
  transfers between devices with their start and end apart: 18, of which 8 were waited for; matrix products, arithmetic and copies ran while one was open for 66% of the time, Pallas kernels for 0%

commit v1 on v0

v1 whole, which is shorter than its diff:
```python
import functools
import math

import jax
import jax.numpy as jnp
from jax import lax
from jax.experimental import pallas as pl
from jax.experimental.pallas import tpu as pltpu
from jax.sharding import PartitionSpec as P

HD = 64
BLK = 64
CHUNK = 4
NEG = -1e30


def plan_blocks(seg, rand, glob):
    rows, full_len = seg.shape
    nb = full_len // BLK
    ids = jnp.arange(nb, dtype=jnp.int32)
    is_global = jnp.any(ids[None, :, None] == glob[:, None, :], axis=-1)
    picked = jnp.any(rand[:, :, None, :] == ids[None, None, :, None], axis=-1)
    nearby = jnp.abs(ids[:, None] - ids[None, :]) <= 1
    admitted = nearby[None] | picked | is_global[:, :, None] | is_global[:, None, :]
    by_block = seg.reshape(rows, nb, BLK)
    low, high = by_block[:, :, 0], by_block[:, :, BLK - 1]
    meets = (low[:, :, None] <= high[:, None, :]) & (low[:, None, :] <= high[:, :, None])
    active = (admitted & meets).astype(jnp.int32)
    upto = (ids[:, None] <= ids[None, :]).astype(jnp.int32)
    place = jnp.sum(active[:, :, :, None] * upto[None, None], axis=2) - 1
    count = jnp.sum(active, axis=2)
    hit = (place[:, :, :, None] == ids[None, None, None, :]) & (active[:, :, :, None] > 0)
    listed = jnp.sum(jnp.where(hit, ids[None, None, :, None], 0), axis=2)
    listed = jnp.where(ids[None, None, :] < count[:, :, None], listed, nb)
    chunks = (count + (CHUNK - 1)) // CHUNK
    seg_cols = jnp.concatenate([seg, jnp.full((rows, BLK), -1, jnp.int32)], axis=1)
    seg_cols = jnp.broadcast_to(seg_cols[:, :, None], (rows, full_len + BLK, 128))
    seg_rows = jnp.concatenate([by_block, by_block], axis=2)[:, :, None, :]
    return chunks, listed.reshape(rows, nb * nb), seg_cols, seg_rows


def lane_low(rows):
    return lax.broadcasted_iota(jnp.int32, (rows, 128), 1) < HD


def diag128(dup_t):
    row = lax.broadcasted_iota(jnp.int32, (128, 128), 0) < HD
    col = lax.broadcasted_iota(jnp.int32, (128, 128), 1) < HD
    return jnp.where(row == col, dup_t, jnp.zeros_like(dup_t))


def transposed_twice(tile):
    both = jnp.concatenate([tile, tile], axis=0)
    return both.T


def head_rows(acc):
    turned = jnp.concatenate([acc, acc], axis=0).T
    return jnp.where(lane_low(HD), turned[:HD], turned[HD:])


def pick_diag(full, half):
    lanes = slice(half * 128, half * 128 + 128)
    top = full[half * 128 : half * 128 + HD, lanes]
    low = full[half * 128 + HD : half * 128 + 128, lanes]
    return jnp.where(lane_low(HD), top, low)


def chunk_ids(list_ref, row, base, nb):
    ids = [list_ref[row, base + j] for j in range(CHUNK)]
    safe = [jnp.where(b == nb, 0, b) for b in ids]
    return ids, safe


def block_rows(ref, blocks, lanes):
    return jnp.concatenate(
        [ref[0, pl.ds(pl.multiple_of(b * BLK, BLK), BLK), lanes] for b in blocks], axis=0
    )


def turned_blocks(ref, blocks, rows):
    low = lane_low(rows.stop - rows.start)
    tiles = [ref[b, rows, :] for b in blocks]
    return jnp.concatenate(
        [jnp.where(low, tiles[i], tiles[i + 1]) for i in range(0, CHUNK, 2)], axis=1
    )


def turn_all(src_ref, dst_ref, nb, width):
    def body(b, _):
        start = pl.multiple_of(b * BLK, BLK)
        for t in range(width // 128):
            tile = src_ref[0, pl.ds(start, BLK), t * 128 : t * 128 + 128]
            dst_ref[b, t * 128 : t * 128 + 128, :] = transposed_twice(tile)
        return 0

    lax.fori_loop(0, nb, body, 0)


def dot_f32(left, right):
    return lax.dot_general(
        left, right, (((1,), (0,)), ((), ())), preferred_element_type=jnp.float32
    )


def forward_kernel(group, n_ref, list_ref, q_ref, k_ref, v_ref, segc_ref, segr_ref,
                   o_ref, lse_ref, vt_ref, qst_ref, m_ref, l_ref, acc_ref):
    row = pl.program_id(0)
    width = q_ref.shape[2]
    nb = q_ref.shape[1] // BLK
    groups, halves = width // group, group // 128
    turn_all(v_ref, vt_ref, nb, width)
    qst_ref[...] = jnp.zeros_like(qst_ref)

    def per_query(a, _):
        start = pl.multiple_of(a * BLK, BLK)
        for t in range(width // 128):
            tile = q_ref[0, pl.ds(start, BLK), t * 128 : t * 128 + 128] * 0.125
            g, u = t // halves, t % halves
            qst_ref[g, u * 128 : u * 128 + 128, u * 128 : u * 128 + 128] = diag128(
                transposed_twice(tile.astype(jnp.bfloat16))
            )
        seg_q = segr_ref[0, a]
        m_ref[...] = jnp.full_like(m_ref, NEG)
        l_ref[...] = jnp.zeros_like(l_ref)
        acc_ref[...] = jnp.zeros_like(acc_ref)

        def per_chunk(c, _):
            ids, safe = chunk_ids(list_ref, row, a * nb + c * CHUNK, nb)
            seg_k = block_rows(segc_ref, ids, slice(0, 128))
            allowed = seg_k == seg_q
            for g in range(groups):
                lanes = slice(g * group, g * group + group)
                s_t = dot_f32(block_rows(k_ref, safe, lanes), qst_ref[g])
                weights, alphas = [], []
                for u in range(halves):
                    t = g * halves + u
                    s = jnp.where(allowed, s_t[:, u * 128 : u * 128 + 128], NEG)
                    m_old = m_ref[t]
                    m_new = jnp.maximum(m_old, jnp.max(s, axis=0, keepdims=True))
                    p = jnp.exp(s - m_new)
                    alpha = jnp.exp(m_old - m_new)
                    l_ref[t] = alpha * l_ref[t] + jnp.sum(p, axis=0, keepdims=True)
                    m_ref[t] = m_new
                    weights.append(p.astype(jnp.bfloat16))
                    alphas.append(alpha)
                p_t = jnp.concatenate(weights, axis=1) if halves > 1 else weights[0]
                o_t = dot_f32(turned_blocks(vt_ref, safe, lanes), p_t)
                for u in range(halves):
                    t = g * halves + u
                    acc_ref[t] = alphas[u] * acc_ref[t] + pick_diag(o_t, u)
            return 0

        lax.fori_loop(0, n_ref[row, a], per_chunk, 0)
        for t in range(width // 128):
            total = l_ref[t]
            out = acc_ref[t] / total
            o_ref[0, pl.ds(start, BLK), t * 128 : t * 128 + 128] = head_rows(out).astype(
                jnp.bfloat16
            )
            lse_ref[0, a, :, t * 128 : t * 128 + 128] = m_ref[t] + jnp.log(total)
        return 0

    lax.fori_loop(0, nb, per_query, 0)


def group_of(width):
    return 256 if width % 256 == 0 else 128


def whole_spec(shape):
    rest = (0,) * (len(shape) - 1)
    return pl.BlockSpec((1,) + tuple(shape[1:]), lambda r, *_: (r,) + rest)


def one_spec(shape):
    rest = (0,) * (len(shape) - 1)
    return pl.BlockSpec((1,) + tuple(shape[1:]), lambda r, *_: (r,) + rest,
                        pipeline_mode=pl.Buffered(1))


def attention_forward(q, k, v, plan):
    chunks, listed, seg_cols, seg_rows = plan
    rows, full_len, width = q.shape
    nb, group = full_len // BLK, group_of(width)
    tiles = width // 128
    pairs = rows * full_len * full_len // 4 * width
    args = (q, k, v, seg_cols, seg_rows)
    return pl.pallas_call(
        functools.partial(forward_kernel, group),
        out_shape=(
            jax.ShapeDtypeStruct((rows, full_len, width), jnp.bfloat16),
            jax.ShapeDtypeStruct((rows, nb, 1, width), jnp.float32),
        ),
        grid_spec=pltpu.PrefetchScalarGridSpec(
            num_scalar_prefetch=2,
            grid=(rows,),
            in_specs=[one_spec(x.shape) for x in args],
            out_specs=(one_spec((rows, full_len, width)), one_spec((rows, nb, 1, width))),
            scratch_shapes=[
                pltpu.VMEM((nb, width, 128), jnp.bfloat16),
                pltpu.VMEM((width // group, group, group), jnp.bfloat16),
                pltpu.VMEM((tiles, 1, 128), jnp.float32),
                pltpu.VMEM((tiles, 1, 128), jnp.float32),
                pltpu.VMEM((tiles, HD, 128), jnp.float32),
            ],
        ),
        compiler_params=pltpu.CompilerParams(vmem_limit_bytes=48 << 20),
        cost_estimate=pl.CostEstimate(
            flops=4 * pairs, transcendentals=pairs // HD, bytes_accessed=8 * q.size
        ),
        name="attention_forward",
    )(chunks, listed, *args)


def backward_kernel(group, n_ref, list_ref, q_ref, k_ref, v_ref, o_ref, do_ref, lse_ref,
                    segc_ref, segr_ref, dq_ref, dk_ref, dv_ref,
                    kt_ref, qst_ref, qs_ref, dost_ref, dos_ref, delta_ref, acc_ref,
                    dk_acc, dv_acc):
    row = pl.program_id(0)
    full_len, width = q_ref.shape[1], q_ref.shape[2]
    nb = full_len // BLK
    groups, halves = width // group, group // 128
    turn_all(k_ref, kt_ref, nb, width)
    for ref in (qst_ref, qs_ref, dost_ref, dos_ref, dk_acc, dv_acc):
        ref[...] = jnp.zeros_like(ref)
    low = lane_low(HD)

    def per_query(a, _):
        start = pl.multiple_of(a * BLK, BLK)
        for t in range(width // 128):
            g, u = t // halves, t % halves
            lanes = slice(t * 128, t * 128 + 128)
            square = slice(u * 128, u * 128 + 128)
            q_tile = (q_ref[0, pl.ds(start, BLK), lanes] * 0.125).astype(jnp.bfloat16)
            g_tile = do_ref[0, pl.ds(start, BLK), lanes]
            o_tile = o_ref[0, pl.ds(start, BLK), lanes]
            g_turn = transposed_twice(g_tile)
            qst_ref[g, square, square] = diag128(transposed_twice(q_tile))
            dost_ref[g, square, square] = diag128(g_turn)
            qs_ref[g, square, square] = diag128(jnp.concatenate([q_tile, q_tile], axis=0))
            dos_ref[g, square, square] = diag128(jnp.concatenate([g_tile, g_tile], axis=0))
            product = g_turn.astype(jnp.float32) * transposed_twice(o_tile).astype(jnp.float32)
            delta_ref[t] = jnp.where(
                low[:1],
                jnp.sum(product[:HD], axis=0, keepdims=True),
                jnp.sum(product[HD:], axis=0, keepdims=True),
            )
        seg_q = segr_ref[0, a]
        acc_ref[...] = jnp.zeros_like(acc_ref)

        def per_chunk(c, _):
            ids, safe = chunk_ids(list_ref, row, a * nb + c * CHUNK, nb)
            seg_k = block_rows(segc_ref, ids, slice(0, 128))
            allowed = seg_k == seg_q
            for g in range(groups):
                lanes = slice(g * group, g * group + group)
                s_t = dot_f32(block_rows(k_ref, safe, lanes), qst_ref[g])
                dp_t = dot_f32(block_rows(v_ref, safe, lanes), dost_ref[g])
                p_parts, ds_parts = [], []
                for u in range(halves):
                    t = g * halves + u
                    half = slice(u * 128, u * 128 + 128)
                    lse = lse_ref[0, a, :, t * 128 : t * 128 + 128]
                    p = jnp.exp(jnp.where(allowed, s_t[:, half], NEG) - lse)
                    ds = p * (dp_t[:, half] - delta_ref[t])
                    p_parts.append(p.astype(jnp.bfloat16))
                    ds_parts.append(ds.astype(jnp.bfloat16))
                p_t = jnp.concatenate(p_parts, axis=1) if halves > 1 else p_parts[0]
                ds_t = jnp.concatenate(ds_parts, axis=1) if halves > 1 else ds_parts[0]
                dv = dot_f32(p_t, dos_ref[g])
                dk = dot_f32(ds_t, qs_ref[g])
                dq_t = dot_f32(turned_blocks(kt_ref, safe, lanes), ds_t)
                for j in range(CHUNK):
                    where = pl.ds(pl.multiple_of(safe[j] * BLK, BLK), BLK)
                    part = slice(j * BLK, j * BLK + BLK)
                    dv_acc[where, lanes] += dv[part]
                    dk_acc[where, lanes] += dk[part]
                for u in range(halves):
                    acc_ref[g * halves + u] += pick_diag(dq_t, u)
            return 0

        lax.fori_loop(0, n_ref[row, a], per_chunk, 0)
        for t in range(width // 128):
            dq_ref[0, pl.ds(start, BLK), t * 128 : t * 128 + 128] = (
                head_rows(acc_ref[t]) * 0.125
            ).astype(jnp.bfloat16)
        return 0

    lax.fori_loop(0, nb, per_query, 0)

    def flush(a, _):
        where = pl.ds(pl.multiple_of(a * BLK, BLK), BLK)
        dk_ref[0, where, :] = dk_acc[where, :].astype(jnp.bfloat16)
        dv_ref[0, where, :] = dv_acc[where, :].astype(jnp.bfloat16)
        return 0

    lax.fori_loop(0, nb, flush, 0)


def attention_backward(q, k, v, o, do, lse, plan):
    chunks, listed, seg_cols, seg_rows = plan
    rows, full_len, width = q.shape
    nb, group = full_len // BLK, group_of(width)
    tiles, groups = width // 128, width // group
    pairs = rows * full_len * full_len // 4 * width
    args = (q, k, v, o, do, lse, seg_cols, seg_rows)
    like = jax.ShapeDtypeStruct((rows, full_len, width), jnp.bfloat16)
    square = pltpu.VMEM((groups, group, group), jnp.bfloat16)
    return pl.pallas_call(
        functools.partial(backward_kernel, group),
        out_shape=(like, like, like),
        grid_spec=pltpu.PrefetchScalarGridSpec(
            num_scalar_prefetch=2,
            grid=(rows,),
            in_specs=[one_spec(x.shape) for x in args],
            out_specs=tuple(one_spec(like.shape) for _ in range(3)),
            scratch_shapes=[
                pltpu.VMEM((nb, width, 128), jnp.bfloat16),
                square, square, square, square,
                pltpu.VMEM((tiles, 1, 128), jnp.float32),
                pltpu.VMEM((tiles, HD, 128), jnp.float32),
                pltpu.VMEM((full_len, width), jnp.float32),
                pltpu.VMEM((full_len, width), jnp.float32),
            ],
        ),
        compiler_params=pltpu.CompilerParams(vmem_limit_bytes=58 << 20),
        cost_estimate=pl.CostEstimate(
            flops=10 * pairs, transcendentals=pairs // HD, bytes_accessed=16 * q.size
        ),
        name="attention_backward",
    )(chunks, listed, *args)


eps_norm = 1e-06


def layer_norm(hidden, gain_vec, shift_vec):
    mean_val = jnp.mean(hidden, axis=-1, keepdims=True)
    centred = hidden - mean_val
    var_val = jnp.mean(centred * centred, axis=-1, keepdims=True)
    return centred * lax.rsqrt(var_val + eps_norm) * gain_vec + shift_vec


def gelu_tanh(values):
    return jax.nn.gelu(values, approximate=True)


def contract_rows(left, right):
    return lax.dot_general(
        left, right, (((0,), (0,)), ((), ())), preferred_element_type=jnp.float32
    )


def times_transpose(left, right):
    return lax.dot_general(
        left, right, (((1,), (1,)), ((), ())), preferred_element_type=jnp.float32
    )


def butterfly_sum(values, axis):
    size = lax.axis_size(axis)
    if size & (size - 1):
        return lax.psum(values, axis)
    step = 1
    while step < size:
        pairs = [(i, i ^ step) for i in range(size)]
        values = values + lax.ppermute(values, axis, pairs)
        step *= 2
    return values


def sum_seq(values):
    if lax.axis_size("seq") == 2:
        other = lax.ppermute(values, "seq", [(0, 1), (1, 0)])
        return values.astype(jnp.float32) + other.astype(jnp.float32)
    return lax.psum(values, "seq").astype(jnp.float32)


class Regroup:
    def __init__(self, row_count):
        self.size = lax.axis_size("seq")
        self.ways = math.gcd(row_count, self.size)
        self.parts = self.size // self.ways
        self.rows = row_count // self.ways
        me = lax.axis_index("seq")
        self.place = lax.rem(me, self.ways)
        self.row_group = me // self.parts

    def targets(self, turn):
        ways, parts = self.ways, self.parts
        return [
            (s, ((s % ways + turn) % ways) * parts + s // ways) for s in range(self.size)
        ]

    def move(self, values, pairs):
        if all(a == b for a, b in pairs):
            return values
        return lax.ppermute(values, "seq", pairs)

    def gather(self, values):
        rows, local, width = self.rows, values.shape[1], values.shape[2]
        out = jnp.zeros((rows, self.ways, local, width), values.dtype)
        for turn in range(self.ways):
            pick = lax.rem(self.place + turn, self.ways)
            chunk = lax.dynamic_slice_in_dim(values, pick * rows, rows, 0)
            chunk = self.move(chunk, self.targets(turn))
            spot = lax.rem(self.row_group - turn + self.ways, self.ways)
            out = lax.dynamic_update_slice_in_dim(out, chunk[:, None], spot, 1)
        return out.reshape(rows, self.ways * local, width)

    def scatter(self, values):
        rows, width = self.rows, values.shape[2]
        local = values.shape[1] // self.ways
        values = values.reshape(rows, self.ways, local, width)
        out = jnp.zeros((rows * self.ways, local, width), values.dtype)
        for turn in range(self.ways):
            spot = lax.rem(self.row_group - turn + self.ways, self.ways)
            chunk = lax.dynamic_slice_in_dim(values, spot, 1, 1)[:, 0]
            chunk = self.move(chunk, [(b, a) for a, b in self.targets(turn)])
            pick = lax.rem(self.place + turn, self.ways)
            out = lax.dynamic_update_slice_in_dim(out, chunk, pick * rows, 0)
        return out

    def pick_rows(self, values):
        return lax.dynamic_slice_in_dim(values, self.row_group * self.rows, self.rows, 0)

    def groups(self):
        return [
            [r * self.parts + j for j in range(self.parts)] for r in range(self.ways)
        ]

    def to_heads(self, values):
        if self.parts == 1:
            return values
        return lax.all_to_all(
            values, "seq", split_axis=2, concat_axis=1, tiled=True,
            axis_index_groups=self.groups(),
        )

    def from_heads(self, values):
        if self.parts == 1:
            return values
        return lax.all_to_all(
            values, "seq", split_axis=1, concat_axis=2, tiled=True,
            axis_index_groups=self.groups(),
        )


def shards(
    tokens_in,
    segment_ids,
    random_blocks,
    global_blocks,
    w_query,
    b_query,
    w_key,
    w_value,
    b_value,
    w_attn_out,
    b_attn_out,
    ln1_gain,
    ln1_bias,
    w_inner,
    b_inner,
    w_outer,
    b_outer,
    ln2_gain,
    ln2_bias,
    out_grad,
):
    row_count, local_len, width = tokens_in.shape
    seq_count = lax.axis_size("seq")
    fsdp_count = lax.axis_size("fsdp")
    tok_count = row_count * local_len
    own = w_query.shape[0]
    per_own = b_inner.shape[0] // own
    regroup = Regroup(row_count)

    vectors = [b_query, b_value, b_attn_out, ln1_gain, ln1_bias, b_outer, ln2_gain, ln2_bias]
    columns = [x[:, None] for x in vectors] + [b_inner.reshape(own, per_own)]
    used = len(vectors) + per_own
    columns.append(jnp.zeros((own, 128 - used), jnp.bfloat16))
    first = jnp.concatenate([w_query, w_key, w_value] + columns, axis=1)
    first = lax.all_gather(first, "fsdp", axis=0, tiled=True)
    qkv_w = first[:, : 3 * width]
    small = first[:, 3 * width : 3 * width + used].astype(jnp.float32).T
    query_b, value_b, out_b, gain_one, bias_one, outer_b, gain_two, bias_two = small[:8]
    inner_b = small[8:].T.reshape(-1)
    second = lax.all_gather(
        jnp.concatenate([w_attn_out, w_inner], axis=1), "fsdp", axis=0, tiled=True
    )
    out_w, inner_w = second[:, :width], second[:, width:]
    outer_w = lax.all_gather(w_outer, "fsdp", axis=0, tiled=True)

    flat_in = regroup.gather(tokens_in).reshape(tok_count, width)
    flat_grad = regroup.gather(out_grad).reshape(tok_count, width)
    plan = plan_blocks(
        regroup.pick_rows(segment_ids),
        regroup.pick_rows(random_blocks),
        regroup.pick_rows(global_blocks),
    )

    def split_rows(values):
        return values.reshape(regroup.rows, tok_count // regroup.rows, width)

    qkv_bias = jnp.concatenate([query_b, jnp.zeros_like(query_b), value_b])
    qkv = (jnp.dot(flat_in, qkv_w, preferred_element_type=jnp.float32) + qkv_bias).astype(
        jnp.bfloat16
    )
    q, k, v = (
        regroup.to_heads(split_rows(qkv[:, i * width : (i + 1) * width])) for i in range(3)
    )
    att, lse = attention_forward(q, k, v, plan)
    att_flat = regroup.from_heads(att).reshape(tok_count, width)
    attn_branch = jnp.dot(att_flat, out_w, preferred_element_type=jnp.float32) + out_b
    resid_one = flat_in.astype(jnp.float32) + attn_branch
    normed_one, norm_one_pull = jax.vjp(layer_norm, resid_one, gain_one, bias_one)
    normed_low = normed_one.astype(jnp.bfloat16)
    inner_pre = jnp.dot(normed_low, inner_w, preferred_element_type=jnp.float32) + inner_b
    inner_act, gelu_pull = jax.vjp(gelu_tanh, inner_pre)
    inner_low = inner_act.astype(jnp.bfloat16)
    mlp_branch = jnp.dot(inner_low, outer_w, preferred_element_type=jnp.float32) + outer_b
    normed_two, norm_two_pull = jax.vjp(layer_norm, normed_one + mlp_branch, gain_two, bias_two)
    out_tokens = regroup.scatter(split_rows(normed_two.astype(jnp.bfloat16)))

    sums = jnp.stack(
        [
            jnp.sum(resid_one * resid_one),
            jnp.sum(attn_branch * attn_branch),
            jnp.sum(mlp_branch * mlp_branch),
        ]
    )
    sums = jnp.broadcast_to(sums[:, None], (3, 128))
    sums = butterfly_sum(butterfly_sum(sums, "fsdp"), "seq")[:, 0]
    rms_values = jnp.sqrt(sums / (tok_count * width * seq_count * fsdp_count))

    def reduced(values):
        return lax.psum_scatter(
            values.astype(jnp.bfloat16), "fsdp", scatter_dimension=0, tiled=True
        )

    d_resid_two, d_gain_two, d_bias_two = norm_two_pull(flat_grad.astype(jnp.float32))
    d_mlp = d_resid_two.astype(jnp.bfloat16)
    d_outer_b = jnp.sum(d_mlp.astype(jnp.float32), axis=0)
    d_outer_w = sum_seq(reduced(contract_rows(inner_low, d_mlp)))
    (d_pre_full,) = gelu_pull(times_transpose(d_mlp, outer_w))
    d_pre = d_pre_full.astype(jnp.bfloat16)
    d_inner_b = jnp.sum(d_pre.astype(jnp.float32), axis=0)
    d_inner_w = contract_rows(normed_low, d_pre)
    d_normed_one = d_resid_two + times_transpose(d_pre, inner_w)
    d_resid_one, d_gain_one, d_bias_one = norm_one_pull(d_normed_one)
    d_attn = d_resid_one.astype(jnp.bfloat16)
    d_out_b = jnp.sum(d_attn.astype(jnp.float32), axis=0)
    d_out_w = contract_rows(att_flat, d_attn)
    d_second = sum_seq(reduced(jnp.concatenate([d_out_w, d_inner_w], axis=1)))
    d_att = times_transpose(d_attn, out_w).astype(jnp.bfloat16)
    dq, dk, dv = attention_backward(
        q, k, v, att, regroup.to_heads(split_rows(d_att)), lse, plan
    )
    dq, dk, dv = (regroup.from_heads(x).reshape(tok_count, width) for x in (dq, dk, dv))
    d_query_b = jnp.sum(dq.astype(jnp.float32), axis=0)
    d_value_b = jnp.sum(dv.astype(jnp.float32), axis=0)
    grads = [
        d_query_b, d_value_b, d_out_b, d_gain_one, d_bias_one, d_outer_b, d_gain_two, d_bias_two,
    ]
    d_small = jnp.concatenate(
        [jnp.stack(grads), d_inner_b.reshape(width, per_own).T,
         jnp.zeros((128 - used, width), jnp.float32)], axis=0
    ).T
    d_first = sum_seq(
        reduced(jnp.concatenate([contract_rows(flat_in, x) for x in (dq, dk, dv)] + [d_small], axis=1))
    )
    d_tokens = d_resid_one
    for i, part in enumerate((dq, dk, dv)):
        d_tokens = d_tokens + times_transpose(part, qkv_w[:, i * width : (i + 1) * width])
    d_tokens_in = regroup.scatter(split_rows(d_tokens.astype(jnp.bfloat16)))
    d_cols = d_first[:, 3 * width :].T
    d_vec = [d_cols[i] for i in range(len(vectors))]
    return (
        out_tokens,
        d_tokens_in,
        d_first[:, :width],
        d_vec[0],
        d_first[:, width : 2 * width],
        d_first[:, 2 * width : 3 * width],
        d_vec[1],
        d_second[:, :width],
        d_vec[2],
        d_vec[3],
        d_vec[4],
        d_second[:, width:],
        d_cols[len(vectors) : used].T.reshape(-1),
        d_outer_w,
        d_vec[5],
        d_vec[6],
        d_vec[7],
        rms_values,
    )


def solution(mesh):
    in_specs = (
        P("fsdp", "seq", None),
        P("fsdp", None),
        P("fsdp", None, None),
        P("fsdp", None),
        P("fsdp", None),
        P("fsdp"),
        P("fsdp", None),
        P("fsdp", None),
        P("fsdp"),
        P("fsdp", None),
        P("fsdp"),
        P("fsdp"),
        P("fsdp"),
        P("fsdp", None),
        P("fsdp"),
        P("fsdp", None),
        P("fsdp"),
        P("fsdp"),
        P("fsdp"),
        P("fsdp", "seq", None),
    )
    out_specs = (
        P("fsdp", "seq", None),
        P("fsdp", "seq", None),
        P("fsdp", None),
        P("fsdp"),
        P("fsdp", None),
        P("fsdp", None),
        P("fsdp"),
        P("fsdp", None),
        P("fsdp"),
        P("fsdp"),
        P("fsdp"),
        P("fsdp", None),
        P("fsdp"),
        P("fsdp", None),
        P("fsdp"),
        P("fsdp"),
        P("fsdp"),
        P(),
    )
    return jax.shard_map(shards, mesh=mesh, in_specs=in_specs, out_specs=out_specs, check_vma=False)
```

time: 2210 us -> 680 us (0.31)
  matrix products: 893 us -> 187 us
  other arithmetic: 343 us -> 34.8 us
  blocking collectives: 301 us -> 0 us
  local copies, waits for them, and re-layouts: 330 us -> 83.5 us
  Pallas kernels: 0 us -> 133 us
  waiting for transfers between devices: 258 us -> 203 us
  loops' own time: 28.1 us -> 0 us
    dot_general x59 -> x1, matrix products: 714 us -> 10.8 us  [shards(): jnp.dot(flat_in, qkv_w, preferred_element_type=jnp.float32) + qkv_bias]
    convert_element_type x32 -> x0, other arithmetic: 185 us -> none  [the longest x8 170 us: step(): d_scores_low = d_scores.astype(jnp.bfloat16)]
    pallas_call x0 -> x2, Pallas kernels: none -> 133 us  [the longest x1 82.4 us: attention_backward(): pl.pallas_call(functools.partial(backward_kernel, group), out_shape=(like...]
    unnamed x2 -> x0, blocking collectives: 126 us -> none
    ppermute x0 -> x12, waiting for transfers between devices: none -> 122 us  [the longest x4 59.6 us: move(): return lax.ppermute(values, 'seq', pairs)]
    reduce_sum x10 -> x5, other arithmetic: 102 us -> 3.7 us  [the longest x1 2.41 us: shards(): d_query_b = jnp.sum(dq.astype(jnp.float32), axis=0)]
    all_to_all x3 -> x0, blocking collectives: 91.5 us -> none  [the longest x1 30.9 us: shards(): lax.all_to_all(from_heads(dv_heads), 'seq', split_axis=1, concat_axis=2,...]
    all_to_all x5 -> x0, waiting for transfers between devices: 85.1 us -> none  [the longest x1 29.5 us: shards(): lax.all_to_all(from_heads(att_heads), 'seq', split_axis=1, concat_axis=2,...]
  transfers between devices with their start and end apart: 18 -> 18, of which waited for: 8 -> 10; matrix products, arithmetic and copies ran while one was open for 66% -> 23% of each run, Pallas kernels for 0% -> 8%
where the time goes in v1:
time: 680 us; the launch traced here: 676 us
  waiting for transfers between devices  203 us (30%)
  matrix products  187 us (28%)
  Pallas kernels  133 us (20%)
  local copies, waits for them, and re-layouts  83.5 us (12%)
  other arithmetic  34.8 us (5%)
  starting transfers between devices  19.2 us (3%)
  between operations  15.2 us (2%)
    pallas_call x1, Pallas kernels, attention_backward(): pl.pallas_call(functools.partial(backward_kernel, group), out_shape=(like...  82.4 us
    reduce_scatter x3, waiting for transfers between devices, reduced(): lax.psum_scatter(values.astype(jnp.bfloat16), 'fsdp', scatter_dimension=0...  81.1 us
    dot_general x6, matrix products, times_transpose(): lax.dot_general(left, right, (((1,), (1,)), ((), ())), preferred_element_...  75.3 us
    ppermute x4, waiting for transfers between devices, move(): return lax.ppermute(values, 'seq', pairs)  59.6 us
    dot_general x6, matrix products, contract_rows(): lax.dot_general(left, right, (((0,), (0,)), ((), ())), preferred_element_...  55.9 us
    ppermute x5, waiting for transfers between devices, butterfly_sum(): values = values + lax.ppermute(values, axis, pairs)  55.2 us
    pallas_call x1, Pallas kernels, attention_forward(): pl.pallas_call(functools.partial(forward_kernel, group), out_shape=(jax.S...  51 us
    unnamed x100, local copies, waits for them, and re-layouts  23.7 us
  transfers between devices with their start and end apart: 18, of which 10 were waited for; matrix products, arithmetic and copies ran while one was open for 23% of the time, Pallas kernels for 8%

profile of v1, /device:TPU:0, one launch (start us, length us, event | category | flops | bytes accessed | tf_op | source)
XLA Modules:
  0.0 676.1 jit_solution(8750733335139266174)
XLA Ops:
  18.0 2.7 constant_dynamic-slice_fusion.4
  20.6 2.9 collective-permute-start
  23.6 2.7 constant_dynamic-slice_fusion
  30.0 2.2 copy-done.20
  32.4 59.6 %collective-permute-done.2 = bf16[1,1024,768]{2,1,0:T(8,128)(2,1)} collective-permute-done((bf16[1,1024,768]{2,1,0:T(8,128)(2,1)}, bf16[1,1024,768]{2,1,0:T(8,128)(2,1)}, u32[]{:S(2)}, u32[]{:S(2)}) %collective-permute-start.2) | collective-permute-done | bytes 1572896 | tf_op jit(solution)/shard_map/ppermute | solution.py:399
  95.0 2.7 bitcast_dynamic-update-slice_fusion.4
  101.5 4.0 slice_reduce_fusion.1
  105.5 10.8 %add_convert_fusion = bf16[2048,2304]{1,0:T(8,128)(2,1)S(1)} fusion(bf16[2048,768]{1,0:T(8,128)(2,1)} %bitcast.149, f32[2304]{0:T(1024)S(1)} %pad_maximum_fusion.3, bf16[768,2432]{1,0:T(8,128)(2,1)} %all-gather.4.cloned.1.call-done), kind=kOutput, calls=%fused_computation.10 | convolution fusion | flops 7257194496 | bytes 16131072 | tf_op jit(solution)/shard_map/dot_general | solution.py:508
  116.3 3.8 slice_bitcast_fusion
  120.5 51.0 %attention_forward.1 = (bf16[1,2048,768]{2,1,0:T(8,128)(2,1)S(1)}, f32[1,32,1,768]{3,2,1,0:T(1,128)S(1)}) custom-call(s32[1,32]{1,0:T(1,128)S(1)} %and_select_fusion.n_ref, s32[1,1024]{1,0:T(1,128)S(1)} %compare_select_fusion.list_ref, bf16[1,2048,768]{2,1,0:T(8,128)(2,1)} %get-tuple-element.134.q_ref, bf16[1,2048,768]{2,1,0:T(8,128)(2,1)} %get-tuple-element.133.k_ref, ...), custom_call_target="tpu_custom_call" | custom-call | flops 3221225472 | bytes 12582912 | tf_op jit(solution)/shard_map/attention_forward/pallas_call | solution.py:189
  173.1 7.8 %fusion.75 = (f32[2048]{0:T(1024)S(1)}, f32[2048,768]{1,0:T(8,128)S(1)}, f32[]{:T(128)}) fusion(f32[768]{0:T(1024)S(1)} %get-tuple-element.111, bf16[1,2,1024,768]{3,2,1,0:T(8,128)(2,1)} %bitcast_dynamic-update-slice_fusion.4, bf16[768,3840]{1,0:T(8,128)(2,1)} %all-gather.6.cloned.1.call-done, bf16[1,2048,768]{2,1,0:T(8,128)(2,1)S(1)} %get-tuple-element.23.o_ref), kind=kOutput, calls=%fused_computation.168 | convolution fusion | flops 2425354240 | bytes 13773828 | tf_op jit(solution)/shard_map/dot_general | solution.py:516
  183.5 20.3 %multiply_convert_fusion = (bf16[2048,3072]{1,0:T(8,128)(2,1)}, f32[2048,3072]{1,0:T(8,128)}) fusion(f32[3072]{0:T(1024)S(1)} %add.240, bf16[768,3840]{1,0:T(8,128)(2,1)S(1)} %bitcast.165, f32[2048,768]{1,0:T(8,128)S(1)} %get-tuple-element.127, f32[768]{0:T(1024)S(1)} %get-tuple-element.109, f32[768]{0:T(1024)S(1)} %get-tuple-element.110, ...), kind=kOutput, calls=%fused_computation.9 | convolution fusion | flops 9734455296 | bytes 48795648 | tf_op jit(solution)/shard_map/dot_general | solution.py:520
  203.7 16.9 %fusion.74 = (f32[2048]{0:T(1024)S(1)}, f32[2048,768]{1,0:T(8,128)S(1)}, f32[]{:T(128)}) fusion(f32[768]{0:T(1024)S(1)} %get-tuple-element.108, f32[768]{0:T(1024)S(1)} %get-tuple-element.109, f32[768]{0:T(1024)S(1)} %get-tuple-element.110, f32[2048]{0:T(1024)S(1)} %fusion.64, f32[2048,768]{1,0:T(8,128)} %copy-done.12, ...), kind=kOutput, calls=%fused_computation.167 | convolution fusion | flops 9677830144 | bytes 29918212 | tf_op jit(solution)/shard_map/dot_general | solution.py:523
  222.5 2.5 fusion.10
  225.1 4.7 fusion.73
  229.8 2.6 copy-done.14
  233.0 30.5 %fusion.79 = (bf16[3072]{0:T(1024)(128)(2,1)S(1)}, bf16[2048,3072]{1,0:T(8,128)(2,1)}) fusion(f32[2048,3072]{1,0:T(8,128)} %get-tuple-element.150, f32[3072]{0:T(1024)S(1)} %add.240, bf16[2048,768]{1,0:T(8,128)(2,1)S(1)} %get-tuple-element.117, bf16[3072,768]{1,0:T(8,128)(2,1)} %all-gather.8.cloned.1.call-done), kind=kOutput, calls=%fused_computation.171 | convolution fusion | flops 9802085376 | bytes 45631488 | tf_op jit(solution)/shard_map/dot_general | solution.py:356
  263.6 19.3 %multiply_reduce_fusion.3 = (bf16[768]{0:T(1024)(128)(2,1)S(1)}, f32[2048]{0:T(1024)S(1)}, f32[]{:T(128)}, bf16[768]{0:T(1024)(128)(2,1)S(1)}, f32[2048,768]{1,0:T(8,128)}) fusion(f32[2048,768]{1,0:T(8,128)S(1)} %bitcast.142, f32[2048]{0:T(1024)S(1)} %fusion.64, f32[2048]{0:T(1024)S(1)} %broadcast_multiply_fusion.1, f32[768]{0:T(1024)S(1)} %get-tuple-element.110, ...), kind=kOutput, calls=%fused_computation.22 | convolution fusion | flops 9682546688 | bytes 36214788 | tf_op jit(solution)/shard_map/dot_general | solution.py:356
  282.9 4.2 fusion.72
  287.8 6.3 fusion.34.do_ref
  294.1 82.4 %attention_backward.1 = (bf16[1,2048,768]{2,1,0:T(8,128)(2,1)}, bf16[1,2048,768]{2,1,0:T(8,128)(2,1)}, bf16[1,2048,768]{2,1,0:T(8,128)(2,1)}) custom-call(s32[1,32]{1,0:T(1,128)} %copy-done.5, s32[1,1024]{1,0:T(1,128)} %copy-done.4, bf16[1,2048,768]{2,1,0:T(8,128)(2,1)} %get-tuple-element.134.q_ref, bf16[1,2048,768]{2,1,0:T(8,128)(2,1)} %get-tuple-element.133.k_ref, ...), custom_call_target="tpu_custom_call" | custom-call | flops 8053063680 | bytes 25165824 | tf_op jit(solution)/shard_map/attention_backward/pallas_call | solution.py:310
  376.5 6.7 fusion.38
  383.2 2.4 reduce.6
  386.2 5.6 fusion.44
  397.1 5.6 fusion.41
  403.4 4.3 concatenate.32
  407.7 3.1 pad_maximum_fusion.1
  410.9 6.1 copy.99
  417.0 15.6 %convolution_convert_fusion = bf16[3072,768]{1,0:T(8,128)(2,1)} fusion(bf16[2048,3072]{1,0:T(8,128)(2,1)} %get-tuple-element.149, bf16[2048,768]{1,0:T(8,128)(2,1)} %copy-done.24), kind=kOutput, calls=%fused_computation.36 | convolution fusion | flops 9666035712 | bytes 20447232 | tf_op jit(solution)/shard_map/dot_general | solution.py:350
  432.7 5.8 fusion.35
  440.3 16.6 %convolution_convert_fusion.1 = bf16[768,3072]{1,0:T(8,128)(2,1)S(1)} fusion(bf16[2048,3072]{1,0:T(8,128)(2,1)} %get-tuple-element.153, f32[2048,768]{1,0:T(8,128)} %copy-done.12, f32[768]{0:T(1024)S(1)} %copy-done.37, f32[768]{0:T(1024)S(1)} %get-tuple-element.110, f32[2048]{0:T(1024)S(1)} %copy-done.32, f32[2048]{0:T(1024)S(1)} %broadcast_multiply_fusion.1), kind=kOutput, calls=%fused_computation.37 | convolution fusion | flops 9673900032 | bytes 23615488 | tf_op jit(solution)/shard_map/dot_general | solution.py:350
  456.9 2.9 pad_maximum_fusion
  461.6 5.9 fusion.28
  467.6 6.0 fusion.24
  473.6 7.3 %add_convert_fusion.1 = bf16[2048,768]{1,0:T(8,128)(2,1)S(1)} fusion(f32[2048,768]{1,0:T(8,128)} %fusion.24, f32[2048,768]{1,0:T(8,128)} %fusion.28, f32[2048,768]{1,0:T(8,128)S(1)} %bitcast.144, bf16[1,2048,768]{2,1,0:T(8,128)(2,1)S(1)} %copy-done.17, f32[2048]{0:T(1024)S(1)} %copy-done.34, bf16[768,2432]{1,0:T(8,128)(2,1)} %all-gather.4.cloned.1.call-done), kind=kOutput, calls=%fused_computation.23 | convolution fusion | flops 2423783424 | bytes 26353664 | tf_op jit(solution)/shard_map/dot_general | solution.py:356
  483.4 2.0 collective-permute-start.1
  485.4 2.0 pad_maximum_fusion.4
  488.9 4.4 collective-permute-done.8
  493.3 4.4 collective-permute-start.9
  497.7 2.2 collective-permute-done.9
  499.9 4.1 collective-permute-start.10
  506.4 2.1 collective-permute-start.11
  508.9 45.7 %collective-permute-done.11 = f32[3,128]{0,1:T(8,128)S(1)} collective-permute-done((f32[3,128]{0,1:T(8,128)S(1)}, f32[3,128]{0,1:T(8,128)S(1)}, u32[]{:S(2)}, u32[]{:S(2)}) %collective-permute-start.11) | collective-permute-done | bytes 1568 | tf_op jit(solution)/shard_map/ppermute | solution.py:368
  555.2 2.9 constant_dynamic-update-slice_fusion
  560.9 2.2 collective-permute-done.4
  568.2 2.9 reduce-scatter.8.cloned.1.call-done
  578.4 78.2 %reduce-scatter.6.cloned.1.call-done = bf16[48,3840]{1,0:T(8,128)(2,1)} async-done(((bf16[768,3840]{1,0:T(8,128)(2,1)}), bf16[48,3840]{1,0:T(8,128)(2,1)}) %reduce-scatter.6.cloned.1.call-update) | async-done | bytes 368656 | tf_op jit(solution)/shard_map/reduce_scatter | solution.py:539
  661.4 5.0 collective-permute-done.5
  (225 shorter events, 69.3 us)
Async XLA Ops:
  7.2 20.6 %copy-start = (s32[2,32,3]{1,0,2:T(2,128)S(1)}, s32[2,32,3]{1,0,2:T(2,128)}, u32[]{:S(2)}) copy-start(s32[2,32,3]{1,0,2:T(2,128)} %param.22) | copy-start | bytes 2308
  7.2 19.6 %copy-start.38 = (s32[2,2048]{1,0:T(2,128)S(1)}, s32[2,2048]{1,0:T(2,128)}, u32[]{:S(2)}) copy-start(s32[2,2048]{1,0:T(2,128)} %param.21) | copy-start | bytes 49156
  7.2 20.7 %copy-start.39 = (s32[2,2]{1,0:T(2,128)S(1)}, s32[2,2]{1,0:T(2,128)}, u32[]{:S(2)}) copy-start(s32[2,2]{1,0:T(2,128)} %param.23) | copy-start | bytes 52
  7.2 90.4 %all-gather.4.cloned.1.call-start = ((), (), s32[]{:S(2)}) async-start(), calls=%async_computation.3 | async-start | bytes 3969024 | tf_op jit(solution)/shard_map/all_gather | solution.py:485
  15.9 13.7 %copy-start.19 = (bf16[2,1024,768]{2,1,0:T(8,128)(2,1)S(1)}, bf16[2,1024,768]{2,1,0:T(8,128)(2,1)}, u32[]{:S(2)}) copy-start(bf16[2,1024,768]{2,1,0:T(8,128)(2,1)} %param.20) | copy-start | bytes 9437188
  15.9 157.2 %all-gather.6.cloned.1.call-start = ((), (), s32[]{:S(2)}) async-start(), calls=%async_computation.4 | async-start | bytes 6266880 | tf_op jit(solution)/shard_map/all_gather | solution.py:490
  17.9 185.8 %all-gather.8.cloned.1.call-start = ((), (), s32[]{:S(2)}) async-start(), calls=%async_computation.5 | async-start | bytes 5013504 | tf_op jit(solution)/shard_map/all_gather | solution.py:494
  20.6 74.4 %collective-permute-start = (bf16[1,1024,768]{2,1,0:T(8,128)(2,1)}, bf16[1,1024,768]{2,1,0:T(8,128)(2,1)}, u32[]{:S(2)}, u32[]{:S(2)}) collective-permute-start(bf16[1,1024,768]{2,1,0:T(8,128)(2,1)} %constant_dynamic-slice_fusion.4), channel_id=1, source_target_pairs={{0,16},{16,0},{1,17},{17,1},{2,18},{18,2},{3,19},{19,3},{4,20},{20... | collective-permute-start | bytes 4718600 | tf_op jit(solution)/shard_map/ppermute | solution.py:399
  26.2 65.8 %collective-permute-start.2 = (bf16[1,1024,768]{2,1,0:T(8,128)(2,1)}, bf16[1,1024,768]{2,1,0:T(8,128)(2,1)}, u32[]{:S(2)}, u32[]{:S(2)}) collective-permute-start(bf16[1,1024,768]{2,1,0:T(8,128)(2,1)} %constant_dynamic-slice_fusion), channel_id=1, source_target_pairs={{0,16},{16,0},{1,17},{17,1},{2,18},{18,2},{3,19},{19,3},{4,20},{20... | collective-permute-start | bytes 4718600 | tf_op jit(solution)/shard_map/ppermute | solution.py:399
  26.2 528.9 %reduce-scatter.10.cloned.1.call-start = ((), (), s32[]{:S(2)}) async-start(), calls=%async_computation.8 | async-start | bytes 3969024 | tf_op jit(solution)/shard_map/reduce_scatter | solution.py:539
  29.3 91.1 %copy-start.3 = (s32[1,32,128]{2,1,0:T(8,128)}, s32[1,32,128]{2,1,0:T(8,128)S(1)}, u32[]{:S(2)}) copy-start(s32[1,32,128]{2,1,0:T(8,128)S(1)} %pad_add_fusion) | copy-start | bytes 49156
  32.4 88.1 %copy-start.5 = (s32[1,32]{1,0:T(1,128)}, s32[1,32]{1,0:T(1,128)S(1)}, u32[]{:S(2)}) copy-start(s32[1,32]{1,0:T(1,128)S(1)} %and_select_fusion.n_ref) | copy-start | bytes 388
  32.4 88.1 %copy-start.4 = (s32[1,1024]{1,0:T(1,128)}, s32[1,1024]{1,0:T(1,128)S(1)}, u32[]{:S(2)}) copy-start(s32[1,1024]{1,0:T(1,128)S(1)} %compare_select_fusion.list_ref) | copy-start | bytes 12292
  93.5 22.8 %copy-start.9 = (bf16[1,2,1024,768]{3,2,1,0:T(8,128)(2,1)}, bf16[1,2,1024,768]{3,2,1,0:T(8,128)(2,1)S(1)}, u32[]{:S(2)}) copy-start(bf16[1,2,1024,768]{3,2,1,0:T(8,128)(2,1)S(1)} %bitcast_dynamic-update-slice_fusion.1) | copy-start | bytes 9437188
  105.5 98.2 %copy-start.36 = (f32[768]{0:T(1024)}, f32[768]{0:T(1024)S(1)}, u32[]{:S(2)}) copy-start(f32[768]{0:T(1024)S(1)} %get-tuple-element.109) | copy-start | bytes 9220
  173.1 7.8 %copy-start.6 = (bf16[1,2048,768]{2,1,0:T(8,128)(2,1)}, bf16[1,2048,768]{2,1,0:T(8,128)(2,1)S(1)}, u32[]{:S(2)}) copy-start(bf16[1,2048,768]{2,1,0:T(8,128)(2,1)S(1)} %get-tuple-element.23.o_ref) | copy-start | bytes 9437188
  173.1 10.3 %slice-start.4 = ((s8[5898240]{0:T(1024)(128)(4,1)}), s8[4194304]{0:T(1024)(128)(4,1)S(1)}, s32[]{:S(2)}) async-start(s8[5898240]{0:T(1024)(128)(4,1)} %bitcast.164), calls=%async_computation.13 | async-start | bytes 8388608
  173.1 10.3 %slice-start.5 = ((s8[5898240]{0:T(1024)(128)(4,1)}), s8[1703936]{0:T(1024)(128)(4,1)S(1)}, s32[]{:S(2)}) async-start(s8[5898240]{0:T(1024)(128)(4,1)} %bitcast.164), calls=%async_computation.14 | async-start | bytes 3407872
  182.8 100.1 %copy-start.31 = (f32[2048]{0:T(1024)}, f32[2048]{0:T(1024)S(1)}, u32[]{:S(2)}) copy-start(f32[2048]{0:T(1024)S(1)} %fusion.64) | copy-start | bytes 24580
  232.4 31.2 %slice-start = ((s8[6291456]{0:T(1024)(128)(4,1)}), s8[4194304]{0:T(1024)(128)(4,1)S(1)}, s32[]{:S(2)}) async-start(s8[6291456]{0:T(1024)(128)(4,1)} %bitcast.141), calls=%async_computation.9 | async-start | bytes 8388608
  233.0 30.6 %copy-start.24 = (bf16[2048,768]{1,0:T(8,128)(2,1)}, bf16[2048,768]{1,0:T(8,128)(2,1)S(1)}, u32[]{:S(2)}) copy-start(bf16[2048,768]{1,0:T(8,128)(2,1)S(1)} %get-tuple-element.117) | copy-start | bytes 9437188
  233.0 30.6 %slice-start.1 = ((s8[6291456]{0:T(1024)(128)(4,1)}), s8[2097152]{0:T(1024)(128)(4,1)S(1)}, s32[]{:S(2)}) async-start(s8[6291456]{0:T(1024)(128)(4,1)} %bitcast.141), calls=%async_computation.10 | async-start | bytes 4194304
  263.6 19.3 %copy-start.30 = (f32[2048]{0:T(1024)S(1)}, f32[2048]{0:T(1024)}, u32[]{:S(2)}) copy-start(f32[2048]{0:T(1024)} %copy-done.29) | copy-start | bytes 24580
  287.2 6.9 %copy-start.13 = (f32[2048,768]{1,0:T(8,128)}, f32[2048,768]{1,0:T(8,128)S(1)}, u32[]{:S(2)}) copy-start(f32[2048,768]{1,0:T(8,128)S(1)} %get-tuple-element.121) | copy-start | bytes 18874372
  287.2 6.9 %copy-start.33 = (f32[2048]{0:T(1024)}, f32[2048]{0:T(1024)S(1)}, u32[]{:S(2)}) copy-start(f32[2048]{0:T(1024)S(1)} %negate_multiply_fusion) | copy-start | bytes 24580
  376.5 9.7 %copy-start.16 = (bf16[1,2048,768]{2,1,0:T(8,128)(2,1)S(1)}, bf16[1,2048,768]{2,1,0:T(8,128)(2,1)}, u32[]{:S(2)}) copy-start(bf16[1,2048,768]{2,1,0:T(8,128)(2,1)} %get-tuple-element.27) | copy-start | bytes 9437188
  397.1 6.3 copy-start.35
  397.1 10.7 %copy-start.26 = (bf16[768,768]{0,1:T(8,128)(2,1)S(1)}, bf16[768,768]{0,1:T(8,128)(2,1)}, u32[]{:S(2)}) copy-start(bf16[768,768]{0,1:T(8,128)(2,1)} %fusion.38) | copy-start | bytes 3538948
  397.1 10.7 %copy-start.27 = (bf16[768,768]{0,1:T(8,128)(2,1)S(1)}, bf16[768,768]{0,1:T(8,128)(2,1)}, u32[]{:S(2)}) copy-start(bf16[768,768]{0,1:T(8,128)(2,1)} %fusion.44) | copy-start | bytes 3538948
  416.9 15.7 %copy-start.7 = (bf16[1,2048,768]{2,1,0:T(8,128)(2,1)S(1)}, bf16[1,2048,768]{2,1,0:T(8,128)(2,1)}, u32[]{:S(2)}) copy-start(bf16[1,2048,768]{2,1,0:T(8,128)(2,1)} %copy-done.6) | copy-start | bytes 9437188
  416.9 154.1 %reduce-scatter.8.cloned.1.call-start = ((), (), s32[]{:S(2)}) async-start(), calls=%async_computation.7 | async-start | bytes 5013504 | tf_op jit(solution)/shard_map/reduce_scatter | solution.py:539
  432.6 7.7 %copy-start.32 = (f32[2048]{0:T(1024)S(1)}, f32[2048]{0:T(1024)}, u32[]{:S(2)}) copy-start(f32[2048]{0:T(1024)} %copy-done.31) | copy-start | bytes 24580
  432.6 7.7 %copy-start.37 = (f32[768]{0:T(1024)S(1)}, f32[768]{0:T(1024)}, u32[]{:S(2)}) copy-start(f32[768]{0:T(1024)} %copy-done.36) | copy-start | bytes 9220
  432.6 223.9 %reduce-scatter.6.cloned.1.call-start = ((), (), s32[]{:S(2)}) async-start(), calls=%async_computation.6 | async-start | bytes 6266880 | tf_op jit(solution)/shard_map/reduce_scatter | solution.py:539
  461.6 11.9 %slice-start.2 = ((s8[6291456]{0:T(1024)(128)(4,1)}), s8[4194304]{0:T(1024)(128)(4,1)S(1)}, s32[]{:S(2)}) async-start(s8[6291456]{0:T(1024)(128)(4,1)} %bitcast.143), calls=%async_computation.11 | async-start | bytes 8388608
  473.6 8.6 %copy-start.15 = (bf16[2048,768]{1,0:T(8,128)(2,1)S(1)}, bf16[2048,768]{1,0:T(8,128)(2,1)}, u32[]{:S(2)}) copy-start(bf16[2048,768]{1,0:T(8,128)(2,1)} %get-tuple-element.135) | copy-start | bytes 9437188
  482.1 73.0 %collective-permute-start.3 = (bf16[1,1024,768]{2,1,0:T(8,128)(2,1)}, bf16[1,1024,768]{2,1,0:T(8,128)(2,1)}, u32[]{:S(2)}, u32[]{:S(2)}) collective-permute-start(bf16[1,1024,768]{2,1,0:T(8,128)(2,1)} %dynamic-slice_bitcast_fusion), channel_id=1, source_target_pairs={{16,0},{0,16},{17,1},{1,17},{18,2},{2,18},{19,3},{3,19},{20,4},{4,... | collective-permute-start | bytes 4718600 | tf_op jit(solution)/shard_map/ppermute | solution.py:399
  483.4 74.7 %collective-permute-start.1 = (bf16[1,1024,768]{2,1,0:T(8,128)(2,1)}, bf16[1,1024,768]{2,1,0:T(8,128)(2,1)}, u32[]{:S(2)}, u32[]{:S(2)}) collective-permute-start(bf16[1,1024,768]{2,1,0:T(8,128)(2,1)} %dynamic-slice_bitcast_fusion.1), channel_id=1, source_target_pairs={{16,0},{0,16},{17,1},{1,17},{18,2},{2,18},{19,3},{3,19},{20,4},{4,... | collective-permute-start | bytes 4718600 | tf_op jit(solution)/shard_map/ppermute | solution.py:399
  487.4 1.4 collective-permute-start.7
  488.9 4.4 collective-permute-start.8
  493.3 6.6 collective-permute-start.9
  499.9 6.5 collective-permute-start.10
  506.4 48.2 %collective-permute-start.11 = (f32[3,128]{0,1:T(8,128)S(1)}, f32[3,128]{0,1:T(8,128)S(1)}, u32[]{:S(2)}, u32[]{:S(2)}) collective-permute-start(f32[3,128]{0,1:T(8,128)S(1)} %add.263), channel_id=1, source_target_pairs={{0,16},{16,0},{1,17},{17,1},{2,18},{18,2},{3,19},{19,3},{4,20},{20... | collective-permute-start | bytes 4616 | tf_op jit(solution)/shard_map/ppermute | solution.py:368
  555.1 8.0 %collective-permute-start.4 = (bf16[48,2432]{1,0:T(8,128)(2,1)}, bf16[48,2432]{1,0:T(8,128)(2,1)}, u32[]{:S(2)}, u32[]{:S(2)}) collective-permute-start(bf16[48,2432]{1,0:T(8,128)(2,1)} %reduce-scatter.10.cloned.1.call-done), channel_id=1, source_target_pairs={{0,16},{16,0},{1,17},{17,1},{2,18},{18,2},{3,19},{19,3},{4,20},{20... | collective-permute-start | bytes 700424 | tf_op jit(solution)/shard_map/ppermute | solution.py:375
  559.6 108.7 %copy-start.21 = (bf16[2,1024,768]{2,1,0:T(8,128)(2,1)}, bf16[2,1024,768]{2,1,0:T(8,128)(2,1)S(1)}, u32[]{:S(2)}) copy-start(bf16[2,1024,768]{2,1,0:T(8,128)(2,1)S(1)} %constant_dynamic-update-slice_fusion.1) | copy-start | bytes 9437188
  559.6 109.4 %copy-start.1 = (s32[2,32,3]{1,0,2:T(2,128)S(1)}, s32[2,32,3]{1,0,2:T(2,128)}, u32[]{:S(2)}) copy-start(s32[2,32,3]{1,0,2:T(2,128)} %param.22) | copy-start | bytes 2308
  571.0 88.5 %collective-permute-start.6 = (bf16[192,768]{1,0:T(8,128)(2,1)}, bf16[192,768]{1,0:T(8,128)(2,1)}, u32[]{:S(2)}, u32[]{:S(2)}) collective-permute-start(bf16[192,768]{1,0:T(8,128)(2,1)} %reduce-scatter.8.cloned.1.call-done), channel_id=1, source_target_pairs={{0,16},{16,0},{1,17},{17,1},{2,18},{18,2},{3,19},{19,3},{4,20},{20... | collective-permute-start | bytes 884744 | tf_op jit(solution)/shard_map/ppermute | solution.py:375
  656.6 9.9 %collective-permute-start.5 = (bf16[48,3840]{1,0:T(8,128)(2,1)}, bf16[48,3840]{1,0:T(8,128)(2,1)S(1)}, u32[]{:S(2)}, u32[]{:S(2)}) collective-permute-start(bf16[48,3840]{1,0:T(8,128)(2,1)} %reduce-scatter.6.cloned.1.call-done), channel_id=1, source_target_pairs={{0,16},{16,0},{1,17},{17,1},{2,18},{18,2},{3,19},{19,3},{4,20},{20... | collective-permute-start | bytes 1105928 | tf_op jit(solution)/shard_map/ppermute | solution.py:375
  (17 other events, 57.1 us)
Sparse Core Ops, SparseCore 0:
  16.0 50.5 all-gather.3
  68.9 58.7 all-gather.5
  130.0 52.0 all-gather.7
  417.1 75.4 reduce-scatter.9
  496.7 74.2 reduce-scatter.7
  574.8 81.6 reduce-scatter.5

commit v2 on v1

--- a/solution.py
+++ b/solution.py
@@ -207,7 +207,7 @@
         ),
         compiler_params=pltpu.CompilerParams(vmem_limit_bytes=48 << 20),
         cost_estimate=pl.CostEstimate(
-            flops=4 * pairs, transcendentals=pairs // HD, bytes_accessed=8 * q.size
+            flops=64 * pairs, transcendentals=pairs // HD, bytes_accessed=8 * q.size
         ),
         name="attention_forward",
     )(chunks, listed, *args)
@@ -326,7 +326,7 @@
         ),
         compiler_params=pltpu.CompilerParams(vmem_limit_bytes=58 << 20),
         cost_estimate=pl.CostEstimate(
-            flops=10 * pairs, transcendentals=pairs // HD, bytes_accessed=16 * q.size
+            flops=100 * pairs, transcendentals=pairs // HD, bytes_accessed=16 * q.size
         ),
         name="attention_backward",
     )(chunks, listed, *args)
@@ -494,7 +494,6 @@
     outer_w = lax.all_gather(w_outer, "fsdp", axis=0, tiled=True)
 
     flat_in = regroup.gather(tokens_in).reshape(tok_count, width)
-    flat_grad = regroup.gather(out_grad).reshape(tok_count, width)
     plan = plan_blocks(
         regroup.pick_rows(segment_ids),
         regroup.pick_rows(random_blocks),
@@ -508,6 +507,8 @@
     qkv = (jnp.dot(flat_in, qkv_w, preferred_element_type=jnp.float32) + qkv_bias).astype(
         jnp.bfloat16
     )
+    qkv, out_grad = lax.optimization_barrier((qkv, out_grad))
+    flat_grad = regroup.gather(out_grad).reshape(tok_count, width)
     q, k, v = (
         regroup.to_heads(split_rows(qkv[:, i * width : (i + 1) * width])) for i in range(3)
     )
@@ -535,15 +536,15 @@
     sums = butterfly_sum(butterfly_sum(sums, "fsdp"), "seq")[:, 0]
     rms_values = jnp.sqrt(sums / (tok_count * width * seq_count * fsdp_count))
 
-    def reduced(values):
-        return lax.psum_scatter(
-            values.astype(jnp.bfloat16), "fsdp", scatter_dimension=0, tiled=True
-        )
+    def scattered(values):
+        return lax.psum_scatter(values, "fsdp", scatter_dimension=0, tiled=True)
 
     d_resid_two, d_gain_two, d_bias_two = norm_two_pull(flat_grad.astype(jnp.float32))
     d_mlp = d_resid_two.astype(jnp.bfloat16)
     d_outer_b = jnp.sum(d_mlp.astype(jnp.float32), axis=0)
-    d_outer_w = sum_seq(reduced(contract_rows(inner_low, d_mlp)))
+    outer_part = contract_rows(inner_low, d_mlp).astype(jnp.bfloat16)
+    d_mlp, outer_part = lax.optimization_barrier((d_mlp, outer_part))
+    d_outer_w = scattered(outer_part)
     (d_pre_full,) = gelu_pull(times_transpose(d_mlp, outer_w))
     d_pre = d_pre_full.astype(jnp.bfloat16)
     d_inner_b = jnp.sum(d_pre.astype(jnp.float32), axis=0)
@@ -553,8 +554,13 @@
     d_attn = d_resid_one.astype(jnp.bfloat16)
     d_out_b = jnp.sum(d_attn.astype(jnp.float32), axis=0)
     d_out_w = contract_rows(att_flat, d_attn)
-    d_second = sum_seq(reduced(jnp.concatenate([d_out_w, d_inner_w], axis=1)))
+    second_part = jnp.concatenate(
+        [d_out_w.astype(jnp.bfloat16), d_inner_w.astype(jnp.bfloat16)], axis=1
+    )
     d_att = times_transpose(d_attn, out_w).astype(jnp.bfloat16)
+    d_att, second_part = lax.optimization_barrier((d_att, second_part))
+    d_outer_w, second_part = lax.optimization_barrier((d_outer_w, second_part))
+    d_second = scattered(second_part)
     dq, dk, dv = attention_backward(
         q, k, v, att, regroup.to_heads(split_rows(d_att)), lse, plan
     )
@@ -568,9 +574,12 @@
         [jnp.stack(grads), d_inner_b.reshape(width, per_own).T,
          jnp.zeros((128 - used, width), jnp.float32)], axis=0
     ).T
-    d_first = sum_seq(
-        reduced(jnp.concatenate([contract_rows(flat_in, x) for x in (dq, dk, dv)] + [d_small], axis=1))
-    )
+    parts = [contract_rows(flat_in, x) for x in (dq, dk, dv)] + [d_small]
+    first_part = jnp.concatenate([x.astype(jnp.bfloat16) for x in parts], axis=1)
+    dq, first_part = lax.optimization_barrier((dq, first_part))
+    d_second, first_part = lax.optimization_barrier((d_second, first_part))
+    d_first = sum_seq(scattered(first_part))
+    d_outer_w, d_second = sum_seq(d_outer_w), sum_seq(d_second)
     d_tokens = d_resid_one
     for i, part in enumerate((dq, dk, dv)):
         d_tokens = d_tokens + times_transpose(part, qkv_w[:, i * width : (i + 1) * width])

time: 680 us -> 569 us (0.84)
  the two profiles are of different devices: /device:TPU:0 before, /device:TPU:16 now
where the time goes in v2:
time: 569 us; the launch traced here: 567 us
  matrix products  182 us (32%)
  Pallas kernels  135 us (24%)
  waiting for transfers between devices  110 us (19%)
  local copies, waits for them, and re-layouts  71.4 us (13%)
  other arithmetic  41.6 us (7%)
  between operations  15.2 us (3%)
  starting transfers between devices  12.5 us (2%)
    pallas_call x1, Pallas kernels, attention_backward(): pl.pallas_call(functools.partial(backward_kernel, group), out_shape=(like...  83.4 us
    dot_general x6, matrix products, times_transpose(): lax.dot_general(left, right, (((1,), (1,)), ((), ())), preferred_element_...  80.6 us
    ppermute x5, waiting for transfers between devices, butterfly_sum(): values = values + lax.ppermute(values, axis, pairs)  62.2 us
    pallas_call x1, Pallas kernels, attention_forward(): pl.pallas_call(functools.partial(forward_kernel, group), out_shape=(jax.S...  51.5 us
    dot_general x6, matrix products, contract_rows(): lax.dot_general(left, right, (((0,), (0,)), ((), ())), preferred_element_...  46.5 us
    ppermute x4, waiting for transfers between devices, move(): return lax.ppermute(values, 'seq', pairs)  27.3 us
    unnamed x86, local copies, waits for them, and re-layouts  24.7 us
    dot_general x1, matrix products, shards(): jnp.dot(normed_low, inner_w, preferred_element_type=jnp.float32) + inner_b  20.9 us
  transfers between devices with their start and end apart: 18, of which 10 were waited for; matrix products, arithmetic and copies ran while one was open for 38% of the time, Pallas kernels for 24%

profile of v2, /device:TPU:16, one launch (start us, length us, event | category | flops | bytes accessed | tf_op | source)
XLA Modules:
  0.0 567.2 jit_solution(10550145308610314831)
XLA Ops:
  17.9 2.7 constant_dynamic-slice_fusion.4
  29.7 27.3 %collective-permute-done = bf16[1,1024,768]{2,1,0:T(8,128)(2,1)} collective-permute-done((bf16[1,1024,768]{2,1,0:T(8,128)(2,1)}, bf16[1,1024,768]{2,1,0:T(8,128)(2,1)}, u32[]{:S(2)}, u32[]{:S(2)}) %collective-permute-start) | collective-permute-done | bytes 1572896 | tf_op jit(solution)/shard_map/ppermute | solution.py:399
  57.0 2.7 bitcast_dynamic-update-slice_fusion.4
  59.7 5.4 all-gather.4.cloned.1.call-done
  67.7 10.5 %add_convert_fusion = bf16[2048,2304]{1,0:T(8,128)(2,1)S(1)} fusion(bf16[2048,768]{1,0:T(8,128)(2,1)} %bitcast.2, f32[2304]{0:T(1024)S(1)} %pad_maximum_fusion.3, bf16[768,2432]{1,0:T(8,128)(2,1)} %all-gather.4.cloned.1.call-done), kind=kOutput, calls=%fused_computation.10 | convolution fusion | flops 7257194496 | bytes 16131072 | tf_op jit(solution)/shard_map/dot_general | solution.py:507
  78.2 4.1 slice_bitcast_fusion
  85.4 51.5 %attention_forward.1 = (bf16[1,2048,768]{2,1,0:T(8,128)(2,1)S(1)}, f32[1,32,1,768]{3,2,1,0:T(1,128)S(1)}) custom-call(s32[1,32]{1,0:T(1,128)S(1)} %and_select_fusion.n_ref, s32[1,1024]{1,0:T(1,128)S(1)} %compare_select_fusion.list_ref, bf16[1,2048,768]{2,1,0:T(8,128)(2,1)} %get-tuple-element.158.q_ref, bf16[1,2048,768]{2,1,0:T(8,128)(2,1)} %get-tuple-element.157.k_ref, ...), custom_call_target="tpu_custom_call" | custom-call | flops 51539607552 | bytes 12582912 | tf_op jit(solution)/shard_map/attention_forward/pallas_call | solution.py:189
  141.9 2.6 bitcast_dynamic-update-slice_fusion.2
  144.5 2.7 bitcast_dynamic-update-slice_fusion.1
  147.2 2.4 reduce.10
  150.2 6.7 %fusion.69 = (f32[2048]{0:T(1024)S(1)}, f32[2048,768]{1,0:T(8,128)S(1)}, f32[]{:T(128)}) fusion(f32[768]{0:T(1024)S(1)} %get-tuple-element.135, bf16[1,2,1024,768]{3,2,1,0:T(8,128)(2,1)} %bitcast_dynamic-update-slice_fusion.4, bf16[768,3840]{1,0:T(8,128)(2,1)} %all-gather.6.cloned.1.call-done, bf16[1,2048,768]{2,1,0:T(8,128)(2,1)S(1)} %get-tuple-element.36.o_ref), kind=kOutput, calls=%fused_computation.165 | convolution fusion | flops 2425354240 | bytes 13773828 | tf_op jit(solution)/shard_map/dot_general | solution.py:517
  159.6 20.9 %multiply_convert_fusion = (bf16[2048,3072]{1,0:T(8,128)(2,1)}, f32[2048,3072]{1,0:T(8,128)}) fusion(f32[3072]{0:T(1024)S(1)} %add.240, bf16[768,3840]{1,0:T(8,128)(2,1)S(1)} %bitcast.158, f32[2048,768]{1,0:T(8,128)S(1)} %get-tuple-element.151, f32[768]{0:T(1024)S(1)} %get-tuple-element.133, f32[768]{0:T(1024)S(1)} %get-tuple-element.134, ...), kind=kOutput, calls=%fused_computation.9 | convolution fusion | flops 9734455296 | bytes 48795648 | tf_op jit(solution)/shard_map/dot_general | solution.py:521
  180.6 16.9 %fusion.68 = (f32[2048]{0:T(1024)S(1)}, f32[2048,768]{1,0:T(8,128)S(1)}, f32[]{:T(128)}) fusion(f32[768]{0:T(1024)S(1)} %get-tuple-element.132, f32[768]{0:T(1024)S(1)} %get-tuple-element.133, f32[768]{0:T(1024)S(1)} %get-tuple-element.134, f32[2048]{0:T(1024)S(1)} %fusion.57, f32[2048,768]{1,0:T(8,128)} %copy-done.10, ...), kind=kOutput, calls=%fused_computation.164 | convolution fusion | flops 9677830144 | bytes 29918212 | tf_op jit(solution)/shard_map/dot_general | solution.py:524
  198.3 4.5 fusion.10
  202.8 7.2 %fusion.67 = (f32[2048]{0:T(1024)S(1)}, f32[2048,768]{1,0:T(8,128)S(1)}, bf16[2048,768]{1,0:T(8,128)(2,1)}) fusion(f32[2048]{0:T(1024)S(1)} %multiply_multiply_fusion.3, f32[2048,768]{1,0:T(8,128)S(1)} %get-tuple-element.149, f32[2048]{0:T(1024)S(1)} %broadcast_multiply_fusion, f32[2048]{0:T(1024)S(1)} %fusion.58, f32[768]{0:T(1024)S(1)} %copy-done.25, ...), kind=kLoop, calls=%fused_computation.163 | loop fusion | flops 18872320 | bytes 18913280 | tf_op jit(solution)/shard_map/transpose(jvp())/reduce_sum | solution.py:340
  210.0 3.2 copy-done.11
  216.0 12.0 %convolution_convert_fusion.1 = bf16[3072,768]{1,0:T(8,128)(2,1)} fusion(bf16[2048,3072]{1,0:T(8,128)(2,1)S(1)} %bitcast.161, bf16[2048,768]{1,0:T(8,128)(2,1)S(1)} %get-tuple-element.38), kind=kOutput, calls=%fused_computation.37 | convolution fusion | flops 9666035712 | bytes 20447232 | tf_op jit(solution)/shard_map/dot_general | solution.py:350
  228.2 33.0 %fusion.73 = (bf16[3072]{0:T(1024)(128)(2,1)S(1)}, bf16[2048,3072]{1,0:T(8,128)(2,1)}) fusion(f32[2048,3072]{1,0:T(8,128)} %get-tuple-element.174, f32[3072]{0:T(1024)S(1)} %add.240, bf16[2048,768]{1,0:T(8,128)(2,1)} %copy-done.19, bf16[3072,768]{1,0:T(8,128)(2,1)} %all-gather.8.cloned.1.call-done), kind=kOutput, calls=%fused_computation.168 | convolution fusion | flops 9802085376 | bytes 45631488 | tf_op jit(solution)/shard_map/dot_general | solution.py:356
  261.2 19.8 %multiply_reduce_fusion.3 = (bf16[768]{0:T(1024)(128)(2,1)S(1)}, f32[2048]{0:T(1024)S(1)}, f32[]{:T(128)}, bf16[768]{0:T(1024)(128)(2,1)S(1)}, f32[2048,768]{1,0:T(8,128)}) fusion(f32[2048,768]{1,0:T(8,128)S(1)} %bitcast.140, f32[2048]{0:T(1024)S(1)} %fusion.57, f32[2048]{0:T(1024)S(1)} %broadcast_multiply_fusion.1, f32[768]{0:T(1024)S(1)} %get-tuple-element.134, ...), kind=kOutput, calls=%fused_computation.23 | convolution fusion | flops 9682546688 | bytes 36214788 | tf_op jit(solution)/shard_map/dot_general | solution.py:356
  281.0 4.2 fusion.66
  285.3 3.2 copy-done.9
  290.8 2.9 fusion.30
  294.3 6.6 %convolution_convert_fusion.2 = bf16[2048,768]{1,0:T(8,128)(2,1)} fusion(bf16[2048,768]{1,0:T(8,128)(2,1)} %copy-done.20, bf16[768,3840]{1,0:T(8,128)(2,1)} %all-gather.6.cloned.1.call-done), kind=kOutput, calls=%fused_computation.44 | convolution fusion | flops 2417491968 | bytes 7471104 | tf_op jit(solution)/shard_map/dot_general | solution.py:356
  300.9 16.6 %convolution_convert_fusion = bf16[768,3072]{1,0:T(8,128)(2,1)S(1)} fusion(bf16[2048,3072]{1,0:T(8,128)(2,1)} %get-tuple-element.177, f32[2048,768]{1,0:T(8,128)} %copy-done.10, f32[768]{0:T(1024)S(1)} %get-tuple-element.133, f32[768]{0:T(1024)S(1)} %get-tuple-element.134, f32[2048]{0:T(1024)S(1)} %fusion.57, f32[2048]{0:T(1024)S(1)} %broadcast_multiply_fusion.1), kind=kOutput, calls=%fused_computation.36 | convolution fusion | flops 9673900032 | bytes 23615488 | tf_op jit(solution)/shard_map/dot_general | solution.py:350
  317.5 2.9 pad_maximum_fusion
  320.5 83.4 %attention_backward.1 = (bf16[1,2048,768]{2,1,0:T(8,128)(2,1)}, bf16[1,2048,768]{2,1,0:T(8,128)(2,1)}, bf16[1,2048,768]{2,1,0:T(8,128)(2,1)}) custom-call(s32[1,32]{1,0:T(1,128)} %copy-done.5, s32[1,1024]{1,0:T(1,128)} %copy-done.4, bf16[1,2048,768]{2,1,0:T(8,128)(2,1)} %get-tuple-element.158.q_ref, bf16[1,2048,768]{2,1,0:T(8,128)(2,1)} %get-tuple-element.157.k_ref, ...), custom_call_target="tpu_custom_call" | custom-call | flops 80530636800 | bytes 25165824 | tf_op jit(solution)/shard_map/attention_backward/pallas_call | solution.py:310
  403.9 2.4 reduce.6
  406.3 2.4 reduce.7
  409.8 5.6 convolution_convert_fusion.3
  415.5 4.8 fusion.36
  420.3 4.6 fusion.33
  424.9 2.3 pad_maximum_fusion.1
  427.2 6.0 %copy.99 = bf16[768,2432]{1,0:T(8,128)(2,1)} copy(bf16[768,2432]{0,1:T(8,128)(2,1)} %pad_maximum_fusion.1) | data formatting | bytes 7471104
  433.2 7.7 %fusion.22 = f32[2048,768]{1,0:T(8,128)} fusion(bf16[1,2048,768]{2,1,0:T(8,128)(2,1)} %get-tuple-element.42, bf16[768,2432]{1,0:T(8,128)(2,1)} %all-gather.4.cloned.1.call-done), kind=kOutput, calls=%fused_computation.48 | convolution fusion | flops 2415919104 | bytes 10616832 | tf_op jit(solution)/shard_map/dot_general | solution.py:356
  440.9 6.0 %fusion.41 = f32[2048,768]{1,0:T(8,128)} fusion(bf16[2048,768]{1,0:T(8,128)(2,1)S(1)} %bitcast.143, bf16[768,2432]{1,0:T(8,128)(2,1)} %all-gather.4.cloned.1.call-done), kind=kOutput, calls=%fused_computation.74 | convolution fusion | flops 2415919104 | bytes 10616832 | tf_op jit(solution)/shard_map/dot_general | solution.py:356
  446.9 7.5 %add_convert_fusion.1 = bf16[2048,768]{1,0:T(8,128)(2,1)S(1)} fusion(f32[2048,768]{1,0:T(8,128)} %fusion.22, f32[2048,768]{1,0:T(8,128)} %fusion.41, f32[2048,768]{1,0:T(8,128)S(1)} %bitcast.138, bf16[1,2048,768]{2,1,0:T(8,128)(2,1)S(1)} %copy-done.13, f32[2048]{0:T(1024)S(1)} %negate_multiply_fusion, bf16[768,2432]{1,0:T(8,128)(2,1)} %all-gather.4.cloned.1.call-done), kind=kOutput, calls=%fused_computation.22 | convolution fusion | flops 2423783424 | bytes 26353664 | tf_op jit(solution)/shard_map/dot_general | solution.py:356
  454.8 2.1 collective-permute-start.1
  456.9 2.0 pad_maximum_fusion.4
  460.3 4.4 collective-permute-done.8
  464.8 5.8 %collective-permute-done.9 = f32[3,128]{0,1:T(8,128)S(1)} collective-permute-done((f32[3,128]{0,1:T(8,128)S(1)}, f32[3,128]{0,1:T(8,128)S(1)}, u32[]{:S(2)}, u32[]{:S(2)}) %collective-permute-start.9) | collective-permute-done | bytes 1568 | tf_op jit(solution)/shard_map/ppermute | solution.py:368
  470.6 4.5 collective-permute-start.10
  475.5 3.9 collective-permute-done.10
  479.9 47.2 %collective-permute-done.11 = f32[3,128]{0,1:T(8,128)S(1)} collective-permute-done((f32[3,128]{0,1:T(8,128)S(1)}, f32[3,128]{0,1:T(8,128)S(1)}, u32[]{:S(2)}, u32[]{:S(2)}) %collective-permute-start.11) | collective-permute-done | bytes 1568 | tf_op jit(solution)/shard_map/ppermute | solution.py:368
  527.8 2.1 collective-permute-start.5
  530.0 7.4 %collective-permute-done.6 = bf16[192,768]{1,0:T(8,128)(2,1)S(1)} collective-permute-done((bf16[192,768]{1,0:T(8,128)(2,1)S(1)}, bf16[192,768]{1,0:T(8,128)(2,1)S(1)}, u32[]{:S(2)}, u32[]{:S(2)}) %collective-permute-start.6) | collective-permute-done | bytes 294944 | tf_op jit(solution)/shard_map/ppermute | solution.py:375
  538.3 7.1 %collective-permute-done.5 = bf16[48,3840]{1,0:T(8,128)(2,1)} collective-permute-done((bf16[48,3840]{1,0:T(8,128)(2,1)S(1)}, bf16[48,3840]{1,0:T(8,128)(2,1)}, u32[]{:S(2)}, u32[]{:S(2)}) %collective-permute-start.5) | collective-permute-done | bytes 368672 | tf_op jit(solution)/shard_map/ppermute | solution.py:375
  548.0 2.0 copy.100
  550.0 2.0 copy.94
  (212 shorter events, 56.5 us)
Async XLA Ops:
  7.2 16.9 %copy-start = (s32[2,32,3]{1,0,2:T(2,128)S(1)}, s32[2,32,3]{1,0,2:T(2,128)}, u32[]{:S(2)}) copy-start(s32[2,32,3]{1,0,2:T(2,128)} %param.22) | copy-start | bytes 2308
  7.2 21.2 %copy-start.15 = (bf16[2,1024,768]{2,1,0:T(8,128)(2,1)S(1)}, bf16[2,1024,768]{2,1,0:T(8,128)(2,1)}, u32[]{:S(2)}) copy-start(bf16[2,1024,768]{2,1,0:T(8,128)(2,1)} %param.20) | copy-start | bytes 9437188
  7.2 57.9 %all-gather.4.cloned.1.call-start = ((), (), s32[]{:S(2)}) async-start(), calls=%async_computation.3 | async-start | bytes 3969024 | tf_op jit(solution)/shard_map/all_gather | solution.py:485
  16.0 134.2 %all-gather.6.cloned.1.call-start = ((), (), s32[]{:S(2)}) async-start(), calls=%async_computation.4 | async-start | bytes 6266880 | tf_op jit(solution)/shard_map/all_gather | solution.py:490
  17.8 162.8 %all-gather.8.cloned.1.call-start = ((), (), s32[]{:S(2)}) async-start(), calls=%async_computation.5 | async-start | bytes 5013504 | tf_op jit(solution)/shard_map/all_gather | solution.py:494
  20.6 36.5 %collective-permute-start = (bf16[1,1024,768]{2,1,0:T(8,128)(2,1)}, bf16[1,1024,768]{2,1,0:T(8,128)(2,1)}, u32[]{:S(2)}, u32[]{:S(2)}) collective-permute-start(bf16[1,1024,768]{2,1,0:T(8,128)(2,1)} %constant_dynamic-slice_fusion.4), channel_id=1, source_target_pairs={{0,16},{16,0},{1,17},{17,1},{2,18},{18,2},{3,19},{19,3},{4,20},{20... | collective-permute-start | bytes 4718600 | tf_op jit(solution)/shard_map/ppermute | solution.py:399
  22.1 298.4 %reduce-scatter.6.cloned.1.call-start = ((), (), s32[]{:S(2)}) async-start(), calls=%async_computation.6 | async-start | bytes 5013504 | tf_op jit(solution)/shard_map/reduce_scatter | solution.py:540
  26.5 58.9 %copy-start.3 = (s32[1,32,128]{2,1,0:T(8,128)}, s32[1,32,128]{2,1,0:T(8,128)S(1)}, u32[]{:S(2)}) copy-start(s32[1,32,128]{2,1,0:T(8,128)S(1)} %pad_add_fusion) | copy-start | bytes 49156
  29.7 55.7 %copy-start.5 = (s32[1,32]{1,0:T(1,128)}, s32[1,32]{1,0:T(1,128)S(1)}, u32[]{:S(2)}) copy-start(s32[1,32]{1,0:T(1,128)S(1)} %and_select_fusion.n_ref) | copy-start | bytes 388
  29.7 55.7 %copy-start.4 = (s32[1,1024]{1,0:T(1,128)}, s32[1,1024]{1,0:T(1,128)S(1)}, u32[]{:S(2)}) copy-start(s32[1,1024]{1,0:T(1,128)S(1)} %compare_select_fusion.list_ref) | copy-start | bytes 12292
  83.6 60.9 %collective-permute-start.2 = (bf16[1,1024,768]{2,1,0:T(8,128)(2,1)}, bf16[1,1024,768]{2,1,0:T(8,128)(2,1)}, u32[]{:S(2)}, u32[]{:S(2)}) collective-permute-start(bf16[1,1024,768]{2,1,0:T(8,128)(2,1)} %constant_dynamic-slice_fusion), channel_id=1, source_target_pairs={{0,16},{16,0},{1,17},{17,1},{2,18},{18,2},{3,19},{19,3},{4,20},{20... | collective-permute-start | bytes 4718600 | tf_op jit(solution)/shard_map/ppermute | solution.py:399
  85.4 51.5 %copy-start.2 = (s32[1,2112,128]{2,1,0:T(8,128)}, s32[1,2112,128]{2,1,0:T(8,128)S(1)}, u32[]{:S(2)}) copy-start(s32[1,2112,128]{2,1,0:T(8,128)S(1)} %broadcast_in_dim.131.segc_ref) | copy-start | bytes 3244036
  137.5 12.7 %copy-start.6 = (bf16[1,2048,768]{2,1,0:T(8,128)(2,1)}, bf16[1,2048,768]{2,1,0:T(8,128)(2,1)S(1)}, u32[]{:S(2)}) copy-start(bf16[1,2048,768]{2,1,0:T(8,128)(2,1)S(1)} %get-tuple-element.36.o_ref) | copy-start | bytes 9437188
  150.2 9.4 %slice-start.4 = ((s8[5898240]{0:T(1024)(128)(4,1)}), s8[4194304]{0:T(1024)(128)(4,1)S(1)}, s32[]{:S(2)}) async-start(s8[5898240]{0:T(1024)(128)(4,1)} %bitcast.157), calls=%async_computation.13 | async-start | bytes 8388608
  150.2 9.4 %slice-start.5 = ((s8[5898240]{0:T(1024)(128)(4,1)}), s8[1703936]{0:T(1024)(128)(4,1)S(1)}, s32[]{:S(2)}) async-start(s8[5898240]{0:T(1024)(128)(4,1)} %bitcast.157), calls=%async_computation.14 | async-start | bytes 3407872
  198.3 4.5 copy-start.26
  202.8 13.2 %slice-start.6 = ((s8[12582912]{0:T(1024)(128)(4,1)}), s8[4194304]{0:T(1024)(128)(4,1)S(1)}, s32[]{:S(2)}) async-start(s8[12582912]{0:T(1024)(128)(4,1)} %bitcast.160), calls=%async_computation.15 | async-start | bytes 8388608
  202.8 13.2 %slice-start.7 = ((s8[12582912]{0:T(1024)(128)(4,1)}), s8[4194304]{0:T(1024)(128)(4,1)S(1)}, s32[]{:S(2)}) async-start(s8[12582912]{0:T(1024)(128)(4,1)} %bitcast.160), calls=%async_computation.16 | async-start | bytes 8388608
  210.0 6.0 %slice-start.8 = ((s8[12582912]{0:T(1024)(128)(4,1)}), s8[4194304]{0:T(1024)(128)(4,1)S(1)}, s32[]{:S(2)}) async-start(s8[12582912]{0:T(1024)(128)(4,1)} %bitcast.160), calls=%async_computation.17 | async-start | bytes 8388608
  228.1 33.1 %slice-start.2 = ((s8[6291456]{0:T(1024)(128)(4,1)}), s8[2097152]{0:T(1024)(128)(4,1)S(1)}, s32[]{:S(2)}) async-start(s8[6291456]{0:T(1024)(128)(4,1)} %bitcast.139), calls=%async_computation.11 | async-start | bytes 4194304
  228.1 199.1 %reduce-scatter.8.cloned.1.call-start = ((), (), s32[]{:S(2)}) async-start(), calls=%async_computation.7 | async-start | bytes 6266880 | tf_op jit(solution)/shard_map/reduce_scatter | solution.py:540
  228.2 33.0 %slice-start.3 = ((s8[6291456]{0:T(1024)(128)(4,1)}), s8[4194304]{0:T(1024)(128)(4,1)S(1)}, s32[]{:S(2)}) async-start(s8[6291456]{0:T(1024)(128)(4,1)} %bitcast.139), calls=%async_computation.12 | async-start | bytes 8388608
  261.2 19.8 %copy-start.24 = (f32[2048]{0:T(1024)S(1)}, f32[2048]{0:T(1024)}, u32[]{:S(2)}) copy-start(f32[2048]{0:T(1024)} %copy-done.23) | copy-start | bytes 24580
  285.2 5.6 copy-start.7
  320.5 217.8 %reduce-scatter.10.cloned.1.call-start = ((), (), s32[]{:S(2)}) async-start(), calls=%async_computation.8 | async-start | bytes 3969024 | tf_op jit(solution)/shard_map/reduce_scatter | solution.py:540
  403.9 5.5 copy-start.28
  403.9 5.5 copy-start.29
  403.9 5.5 copy-start.27
  409.8 5.7 copy-start.13
  415.5 4.8 copy-start.30
  433.2 7.7 %copy-start.14 = (bf16[1,2048,768]{2,1,0:T(8,128)(2,1)S(1)}, bf16[1,2048,768]{2,1,0:T(8,128)(2,1)}, u32[]{:S(2)}) copy-start(bf16[1,2048,768]{2,1,0:T(8,128)(2,1)} %get-tuple-element.41) | copy-start | bytes 9437188
  433.2 13.7 %slice-start = ((s8[6291456]{0:T(1024)(128)(4,1)}), s8[4194304]{0:T(1024)(128)(4,1)S(1)}, s32[]{:S(2)}) async-start(s8[6291456]{0:T(1024)(128)(4,1)} %bitcast.137), calls=%async_computation.9 | async-start | bytes 8388608
  440.9 6.0 %slice-start.1 = ((s8[6291456]{0:T(1024)(128)(4,1)}), s8[2097152]{0:T(1024)(128)(4,1)S(1)}, s32[]{:S(2)}) async-start(s8[6291456]{0:T(1024)(128)(4,1)} %bitcast.137), calls=%async_computation.10 | async-start | bytes 4194304
  446.9 7.7 %copy-start.12 = (bf16[2048,768]{1,0:T(8,128)(2,1)S(1)}, bf16[2048,768]{1,0:T(8,128)(2,1)}, u32[]{:S(2)}) copy-start(bf16[2048,768]{1,0:T(8,128)(2,1)} %get-tuple-element.159) | copy-start | bytes 9437188
  454.6 73.0 %collective-permute-start.3 = (bf16[1,1024,768]{2,1,0:T(8,128)(2,1)S(1)}, bf16[1,1024,768]{2,1,0:T(8,128)(2,1)S(1)}, u32[]{:S(2)}, u32[]{:S(2)}) collective-permute-start(bf16[1,1024,768]{2,1,0:T(8,128)(2,1)S(1)} %dynamic-slice_bitcast_fusion), channel_id=1, source_target_pairs={{16,0},{0,16},{17,1},{1,17},{18,2},{2,18},{19,3},{3,19},{20,4},{4,... | collective-permute-start | bytes 4718600 | tf_op jit(solution)/shard_map/ppermute | solution.py:399
  454.8 75.1 %collective-permute-start.1 = (bf16[1,1024,768]{2,1,0:T(8,128)(2,1)S(1)}, bf16[1,1024,768]{2,1,0:T(8,128)(2,1)S(1)}, u32[]{:S(2)}, u32[]{:S(2)}) collective-permute-start(bf16[1,1024,768]{2,1,0:T(8,128)(2,1)S(1)} %dynamic-slice_bitcast_fusion.1), channel_id=1, source_target_pairs={{16,0},{0,16},{17,1},{1,17},{18,2},{2,18},{19,3},{3,19},{20,4},{4,... | collective-permute-start | bytes 4718600 | tf_op jit(solution)/shard_map/ppermute | solution.py:399
  458.9 1.4 collective-permute-start.7
  460.2 4.4 collective-permute-start.8
  464.7 5.9 %collective-permute-start.9 = (f32[3,128]{0,1:T(8,128)S(1)}, f32[3,128]{0,1:T(8,128)S(1)}, u32[]{:S(2)}, u32[]{:S(2)}) collective-permute-start(f32[3,128]{0,1:T(8,128)S(1)} %fusion.89), channel_id=1, source_target_pairs={{0,4},{1,5},{2,6},{3,7},{4,0},{5,1},{6,2},{7,3},{8,12},{9,13},{10,... | collective-permute-start | bytes 4616 | tf_op jit(solution)/shard_map/ppermute | solution.py:368
  470.6 57.0 %copy-start.22 = (bf16[192,768]{1,0:T(8,128)(2,1)S(1)}, bf16[192,768]{1,0:T(8,128)(2,1)}, u32[]{:S(2)}) copy-start(bf16[192,768]{1,0:T(8,128)(2,1)} %reduce-scatter.6.cloned.1.call-done) | copy-start | bytes 884740
  470.6 8.8 %collective-permute-start.10 = (f32[3,128]{0,1:T(8,128)S(1)}, f32[3,128]{0,1:T(8,128)S(1)}, u32[]{:S(2)}, u32[]{:S(2)}) collective-permute-start(f32[3,128]{0,1:T(8,128)S(1)} %add.262), channel_id=1, source_target_pairs={{0,8},{1,9},{2,10},{3,11},{4,12},{5,13},{6,14},{7,15},{8,0},{9,1},... | collective-permute-start | bytes 4616 | tf_op jit(solution)/shard_map/ppermute | solution.py:368
  475.3 52.5 %copy-start.21 = (bf16[48,3840]{1,0:T(8,128)(2,1)S(1)}, bf16[48,3840]{1,0:T(8,128)(2,1)}, u32[]{:S(2)}) copy-start(bf16[48,3840]{1,0:T(8,128)(2,1)} %reduce-scatter.8.cloned.1.call-done) | copy-start | bytes 1105924
  479.4 47.6 %collective-permute-start.11 = (f32[3,128]{0,1:T(8,128)S(1)}, f32[3,128]{0,1:T(8,128)S(1)}, u32[]{:S(2)}, u32[]{:S(2)}) collective-permute-start(f32[3,128]{0,1:T(8,128)S(1)} %add.263), channel_id=1, source_target_pairs={{0,16},{16,0},{1,17},{17,1},{2,18},{18,2},{3,19},{19,3},{4,20},{20... | collective-permute-start | bytes 4616 | tf_op jit(solution)/shard_map/ppermute | solution.py:368
  527.5 9.9 %collective-permute-start.6 = (bf16[192,768]{1,0:T(8,128)(2,1)S(1)}, bf16[192,768]{1,0:T(8,128)(2,1)S(1)}, u32[]{:S(2)}, u32[]{:S(2)}) collective-permute-start(bf16[192,768]{1,0:T(8,128)(2,1)S(1)} %copy-done.22), channel_id=1, source_target_pairs={{0,16},{16,0},{1,17},{17,1},{2,18},{18,2},{3,19},{19,3},{4,20},{20... | collective-permute-start | bytes 884744 | tf_op jit(solution)/shard_map/ppermute | solution.py:375
  527.8 17.7 %collective-permute-start.5 = (bf16[48,3840]{1,0:T(8,128)(2,1)S(1)}, bf16[48,3840]{1,0:T(8,128)(2,1)}, u32[]{:S(2)}, u32[]{:S(2)}) collective-permute-start(bf16[48,3840]{1,0:T(8,128)(2,1)S(1)} %copy-done.21), channel_id=1, source_target_pairs={{0,16},{16,0},{1,17},{17,1},{2,18},{18,2},{3,19},{19,3},{4,20},{20... | collective-permute-start | bytes 1105928 | tf_op jit(solution)/shard_map/ppermute | solution.py:375
  530.0 28.5 %copy-start.17 = (bf16[2,1024,768]{2,1,0:T(8,128)(2,1)}, bf16[2,1024,768]{2,1,0:T(8,128)(2,1)S(1)}, u32[]{:S(2)}) copy-start(bf16[2,1024,768]{2,1,0:T(8,128)(2,1)S(1)} %constant_dynamic-update-slice_fusion.1) | copy-start | bytes 9437188
  537.4 22.7 %copy-start.1 = (s32[2,32,3]{1,0,2:T(2,128)S(1)}, s32[2,32,3]{1,0,2:T(2,128)}, u32[]{:S(2)}) copy-start(s32[2,32,3]{1,0,2:T(2,128)} %param.22) | copy-start | bytes 2308
  538.3 11.7 %collective-permute-start.4 = (bf16[48,2432]{1,0:T(8,128)(2,1)}, bf16[48,2432]{1,0:T(8,128)(2,1)}, u32[]{:S(2)}, u32[]{:S(2)}) collective-permute-start(bf16[48,2432]{1,0:T(8,128)(2,1)} %reduce-scatter.10.cloned.1.call-done), channel_id=1, source_target_pairs={{0,16},{16,0},{1,17},{17,1},{2,18},{18,2},{3,19},{19,3},{4,20},{20... | collective-permute-start | bytes 700424 | tf_op jit(solution)/shard_map/ppermute | solution.py:375
  (10 other events, 21.4 us)
Sparse Core Ops, SparseCore 0:
  16.2 48.8 all-gather.3
  67.9 58.3 all-gather.5
  128.6 51.9 all-gather.7
  228.2 73.6 reduce-scatter.5
  320.6 81.0 reduce-scatter.7
  433.3 71.4 reduce-scatter.9
